TPU v7x, 32 devices: a whole 2x2x4 slice. The times are simulated.
32 devices in a mesh: seq: 4 (over x, core), ctx: 4 (over z), fsdp: 2 (over y).
Axes of the slice: x: 2, y: 2, z: 4, core: 2. Of those that a mesh axis runs over, the one named last changes fastest.
Arguments:
- hidden_in: bfloat16 [8, 512, 768], P(('seq', 'fsdp'), 'ctx'), may hold values from -6 to 6
- encoder_states: bfloat16 [8, 64, 768], P(('seq', 'fsdp'), 'ctx'), may hold values from -6 to 6
- out_grad: bfloat16 [8, 512, 768], P(('seq', 'fsdp'), 'ctx'), may hold values from -6 to 6
- bucket_index: int32 [512], replicated, may hold values from 0 to 31, as said below
- bias_table: float32 [32, 12], replicated, may hold values from -5 to 5
- self_gain: bfloat16 [768], P(('ctx', 'fsdp')), may hold values from 0.099609375 to 1.8984375
- self_query: bfloat16 [768, 768], P(('ctx', 'fsdp')), may hold values from -0.02734375 to 0.02734375
- self_key: bfloat16 [768, 768], P(('ctx', 'fsdp')), may hold values from -0.21875 to 0.21875
- self_value: bfloat16 [768, 768], P(('ctx', 'fsdp')), may hold values from -0.21875 to 0.21875
- self_output: bfloat16 [768, 768], P(('ctx', 'fsdp')), may hold values from -1.5 to 1.5
- cross_gain: bfloat16 [768], P(('ctx', 'fsdp')), may hold values from 0.099609375 to 1.8984375
- cross_query: bfloat16 [768, 768], P(('ctx', 'fsdp')), may hold values from -0.02734375 to 0.02734375
- cross_key: bfloat16 [768, 768], P(('ctx', 'fsdp')), may hold values from -0.21875 to 0.21875
- cross_value: bfloat16 [768, 768], P(('ctx', 'fsdp')), may hold values from -0.21875 to 0.21875
- cross_output: bfloat16 [768, 768], P(('ctx', 'fsdp')), may hold values from -1.5 to 1.5
- feed_gain: bfloat16 [768], P(('ctx', 'fsdp')), may hold values from 0.099609375 to 1.8984375
- gate_weight: bfloat16 [768, 2048], P(('ctx', 'fsdp')), may hold values from -0.21875 to 0.21875
- linear_weight: bfloat16 [768, 2048], P(('ctx', 'fsdp')), may hold values from -0.21875 to 0.21875
- down_weight: bfloat16 [2048, 768], P(('ctx', 'fsdp')), may hold values from -0.125 to 0.125
Outputs:
- layer_out: bfloat16 [8, 512, 768], P(('seq', 'fsdp'), 'ctx')
- input_grad: float32 [8, 512, 768], P(('seq', 'fsdp'), 'ctx')
- encoder_grad: float32 [8, 64, 768], P(('seq', 'fsdp'), 'ctx')
- grad_bias_table: float32 [32, 12], replicated
- grad_self_gain: float32 [768], P(('ctx', 'fsdp'))
- grad_self_query: float32 [768, 768], P(('ctx', 'fsdp'))
- grad_self_key: float32 [768, 768], P(('ctx', 'fsdp'))
- grad_self_value: float32 [768, 768], P(('ctx', 'fsdp'))
- grad_self_output: float32 [768, 768], P(('ctx', 'fsdp'))
- grad_cross_gain: float32 [768], P(('ctx', 'fsdp'))
- grad_cross_query: float32 [768, 768], P(('ctx', 'fsdp'))
- grad_cross_key: float32 [768, 768], P(('ctx', 'fsdp'))
- grad_cross_value: float32 [768, 768], P(('ctx', 'fsdp'))
- grad_cross_output: float32 [768, 768], P(('ctx', 'fsdp'))
- grad_feed_gain: float32 [768], P(('ctx', 'fsdp'))
- grad_gate_weight: float32 [768, 2048], P(('ctx', 'fsdp'))
- grad_linear_weight: float32 [768, 2048], P(('ctx', 'fsdp'))
- grad_down_weight: float32 [2048, 768], P(('ctx', 'fsdp'))
Inputs may be any that keep to these rules, and one draw needn't show every extreme that they name: bucket_index[d] is the bucket of a key that lies d positions before its query; it is 0 at d = 0 and never falls as d grows.
All inputs are finite; a program needn't handle non-finite values.
Results may differ from a plain program's by a relative error of at most 0.025.
Values may be sent and summed in bfloat16 or wider, within the bound.
A program may use at most 256 MiB of HBM per device.

v0:
```python
from functools import partial
import math

import jax
import jax.numpy as jnp
from jax import lax
from jax.sharding import PartitionSpec as P

EPSILON = 1e-06
NEGATIVE = -1e30
HIGHEST = lax.Precision.HIGHEST


def product(left, right):
    return jnp.dot(left, right, preferred_element_type=jnp.float32)


def row_contract(left, right):
    return lax.dot_general(
        left, right, (((0,), (0,)), ((), ())), preferred_element_type=jnp.float32
    )


def col_contract(left, right):
    return lax.dot_general(
        left, right, (((1,), (1,)), ((), ())), preferred_element_type=jnp.float32
    )


def norm_forward(values, gain):
    inverse = lax.rsqrt(jnp.mean(values * values, axis=-1, keepdims=True) + EPSILON)
    normed = values * inverse
    return ((normed * gain.astype(jnp.float32)).astype(jnp.bfloat16), normed, inverse)


def norm_backward(upstream, normed, inverse, gain):
    grad_gain = jnp.sum(upstream * normed, axis=0)
    grad_normed = upstream * gain.astype(jnp.float32)
    grad_values = inverse * (
        grad_normed - normed * jnp.mean(grad_normed * normed, axis=-1, keepdims=True)
    )
    return (grad_values, grad_gain)


def geglu(gate_pre, linear_pre):
    return jax.nn.gelu(gate_pre, approximate=True) * linear_pre


def by_heads(values, head_count):
    return values.reshape(values.shape[0], head_count, values.shape[1] // head_count)


def band_onehot(bucket_rev, buckets, query_rows, key_rows, query_first, key_first):
    length = bucket_rev.shape[0] // 2
    offset_first = query_first - key_first
    upper_band = lax.dynamic_slice_in_dim(bucket_rev, length - 1 - offset_first, key_rows, 0)
    lower_band = lax.dynamic_slice_in_dim(
        bucket_rev, length - offset_first - query_rows, query_rows - 1, 0
    )
    slots = jnp.concatenate([upper_band, jnp.full((1,), -1, jnp.int32), lower_band])
    return (slots[:, None] == jnp.arange(buckets, dtype=jnp.int32)[None, :]).astype(jnp.float32)


def spread_band(band, query_rows, key_rows):
    head_count, width = band.shape
    tiled = jnp.broadcast_to(band[:, None, :], (head_count, query_rows, width)).reshape(
        head_count, query_rows * width
    )
    return tiled[:, : query_rows * (width - 1)].reshape(head_count, query_rows, width - 1)[
        :, :, :key_rows
    ]


def fold_band(grad_scores, width):
    head_count, query_rows, key_rows = grad_scores.shape
    padded = jnp.pad(grad_scores, ((0, 0), (0, 0), (0, width - 1 - key_rows))).reshape(
        head_count, query_rows * (width - 1)
    )
    padded = jnp.pad(padded, ((0, 0), (0, query_rows)))
    return jnp.sum(padded.reshape(head_count, query_rows, width), axis=1)


def self_scores(query, key_block, query_first, key_first, bucket_rev, bias_table):
    head_count = bias_table.shape[1]
    query_rows = query.shape[0]
    key_rows = key_block.shape[0]
    scores = jnp.einsum(
        "qhe,khe->hqk",
        by_heads(query, head_count),
        by_heads(key_block, head_count),
        preferred_element_type=jnp.float32,
    )
    offset = (query_first + jnp.arange(query_rows, dtype=jnp.int32))[:, None] - (
        key_first + jnp.arange(key_rows, dtype=jnp.int32)
    )[None, :]
    allowed = offset >= 0
    onehot = band_onehot(
        bucket_rev, bias_table.shape[0], query_rows, key_rows, query_first, key_first
    )
    band = jnp.dot(onehot, bias_table, precision=HIGHEST).T
    scores = jnp.where(allowed[None], scores + spread_band(band, query_rows, key_rows), NEGATIVE)
    return (scores, allowed, onehot)


def table_terms(grad_scores, onehot):
    band_grad = fold_band(grad_scores, onehot.shape[0])
    return jnp.dot(onehot.T, band_grad.T, precision=HIGHEST)


def fold_blocks(block_step, running, arrays, first_row):
    piece_rows = arrays[0].shape[0]
    block_size = math.gcd(piece_rows, 512) if piece_rows > 512 else piece_rows
    if block_size == piece_rows:
        return block_step(running, arrays, first_row)
    block_count = piece_rows // block_size
    stacked = tuple(
        (member.reshape((block_count, block_size) + member.shape[1:]) for member in arrays)
    )

    def scan_block(state_now, scanned):
        number, blocks = scanned
        return (block_step(state_now, blocks, first_row + number * block_size), None)

    result, _ = lax.scan(scan_block, running, (jnp.arange(block_count, dtype=jnp.int32), stacked))
    return result


def forward_step(running, blocks, key_first, query, query_first, bucket_rev, bias_table):
    top, total, mixed = running
    key_block, value_block = blocks
    head_count = bias_table.shape[1]
    scores, allowed, _ = self_scores(
        query, key_block, query_first, key_first, bucket_rev, bias_table
    )
    new_top = jnp.maximum(top, jnp.max(scores, axis=-1))
    weights = jnp.where(allowed[None], jnp.exp(scores - new_top[:, :, None]), 0.0)
    rescale = jnp.exp(top - new_top)
    total = total * rescale + jnp.sum(weights, axis=-1)
    update = jnp.einsum(
        "hqk,khe->qhe",
        weights.astype(jnp.bfloat16),
        by_heads(value_block, head_count),
        preferred_element_type=jnp.float32,
    )
    mixed = mixed * rescale.T[:, :, None] + update
    return (new_top, total, mixed)


def backward_core(
    query,
    grad_attn,
    lse_rows,
    delta_rows,
    key_block,
    value_block,
    query_first,
    key_first,
    bucket_rev,
    bias_table,
):
    head_count = bias_table.shape[1]
    scores, allowed, onehot = self_scores(
        query, key_block, query_first, key_first, bucket_rev, bias_table
    )
    probs = jnp.where(allowed[None], jnp.exp(scores - lse_rows.T[:, :, None]), 0.0)
    grad_probs = jnp.einsum(
        "qhe,khe->hqk",
        by_heads(grad_attn, head_count),
        by_heads(value_block, head_count),
        preferred_element_type=jnp.float32,
    )
    grad_scores = probs * (grad_probs - delta_rows.T[:, :, None])
    return (probs, grad_scores, onehot)


def partial_step(
    running,
    blocks,
    key_first,
    query,
    grad_attn,
    lse_rows,
    delta_rows,
    query_first,
    bucket_rev,
    bias_table,
):
    grad_query, grad_keys, grad_values, table_part = running
    key_block, value_block = blocks
    head_count = bias_table.shape[1]
    probs, grad_scores, onehot = backward_core(
        query,
        grad_attn,
        lse_rows,
        delta_rows,
        key_block,
        value_block,
        query_first,
        key_first,
        bucket_rev,
        bias_table,
    )
    rounded = grad_scores.astype(jnp.bfloat16)
    grad_query = grad_query + jnp.einsum(
        "hqk,khe->qhe", rounded, by_heads(key_block, head_count), preferred_element_type=jnp.float32
    )
    key_part = jnp.einsum(
        "hqk,qhe->khe", rounded, by_heads(query, head_count), preferred_element_type=jnp.float32
    ).reshape(key_block.shape[0], -1)
    value_part = jnp.einsum(
        "hqk,qhe->khe",
        probs.astype(jnp.bfloat16),
        by_heads(grad_attn, head_count),
        preferred_element_type=jnp.float32,
    ).reshape(key_block.shape[0], -1)
    grad_keys = lax.dynamic_update_slice_in_dim(grad_keys, key_part, key_first, 0)
    grad_values = lax.dynamic_update_slice_in_dim(grad_values, value_part, key_first, 0)
    table_part = table_part + table_terms(grad_scores, onehot)
    return (grad_query, grad_keys, grad_values, table_part)


def plain_forward(query, keys, values, head_count):
    scores = jnp.einsum(
        "qhe,khe->hqk",
        by_heads(query, head_count),
        by_heads(keys, head_count),
        preferred_element_type=jnp.float32,
    )
    top = jnp.max(scores, axis=-1, keepdims=True)
    weights = jnp.exp(scores - top)
    total = jnp.sum(weights, axis=-1, keepdims=True)
    mixed = jnp.einsum(
        "hqk,khe->qhe",
        weights.astype(jnp.bfloat16),
        by_heads(values, head_count),
        preferred_element_type=jnp.float32,
    )
    result = (
        (mixed / jnp.transpose(total, (1, 0, 2))).reshape(query.shape[0], -1).astype(jnp.bfloat16)
    )
    return (result, (top + jnp.log(total))[:, :, 0])


def plain_backward(query, keys, values, lse, output, grad_output, head_count):
    split_grad = by_heads(grad_output, head_count)
    delta = jnp.sum(
        split_grad.astype(jnp.float32) * by_heads(output, head_count).astype(jnp.float32), axis=-1
    ).T
    scores = jnp.einsum(
        "qhe,khe->hqk",
        by_heads(query, head_count),
        by_heads(keys, head_count),
        preferred_element_type=jnp.float32,
    )
    probs = jnp.exp(scores - lse[:, :, None])
    grad_probs = jnp.einsum(
        "qhe,khe->hqk", split_grad, by_heads(values, head_count), preferred_element_type=jnp.float32
    )
    rounded = (probs * (grad_probs - delta[:, :, None])).astype(jnp.bfloat16)
    grad_query = jnp.einsum(
        "hqk,khe->qhe", rounded, by_heads(keys, head_count), preferred_element_type=jnp.float32
    ).reshape(query.shape[0], -1)
    grad_keys = jnp.einsum(
        "hqk,qhe->khe", rounded, by_heads(query, head_count), preferred_element_type=jnp.float32
    ).reshape(keys.shape[0], -1)
    grad_values = jnp.einsum(
        "hqk,qhe->khe", probs.astype(jnp.bfloat16), split_grad, preferred_element_type=jnp.float32
    ).reshape(keys.shape[0], -1)
    return (grad_query, grad_keys, grad_values)


def per_device(
    hidden_in,
    encoder_states,
    out_grad,
    bucket_index,
    bias_table,
    self_gain,
    self_query,
    self_key,
    self_value,
    self_output,
    cross_gain,
    cross_query,
    cross_key,
    cross_value,
    cross_output,
    feed_gain,
    gate_weight,
    linear_weight,
    down_weight,
):
    (
        self_gain,
        self_query,
        self_key,
        self_value,
        self_output,
        cross_gain,
        cross_query,
        cross_key,
        cross_value,
        cross_output,
        feed_gain,
        gate_weight,
        linear_weight,
        down_weight,
    ) = (
        lax.all_gather(self_gain, ("ctx", "fsdp"), axis=0, tiled=True),
        lax.all_gather(self_query, ("ctx", "fsdp"), axis=0, tiled=True),
        lax.all_gather(self_key, ("ctx", "fsdp"), axis=0, tiled=True),
        lax.all_gather(self_value, ("ctx", "fsdp"), axis=0, tiled=True),
        lax.all_gather(self_output, ("ctx", "fsdp"), axis=0, tiled=True),
        lax.all_gather(cross_gain, ("ctx", "fsdp"), axis=0, tiled=True),
        lax.all_gather(cross_query, ("ctx", "fsdp"), axis=0, tiled=True),
        lax.all_gather(cross_key, ("ctx", "fsdp"), axis=0, tiled=True),
        lax.all_gather(cross_value, ("ctx", "fsdp"), axis=0, tiled=True),
        lax.all_gather(cross_output, ("ctx", "fsdp"), axis=0, tiled=True),
        lax.all_gather(feed_gain, ("ctx", "fsdp"), axis=0, tiled=True),
        lax.all_gather(gate_weight, ("ctx", "fsdp"), axis=0, tiled=True),
        lax.all_gather(linear_weight, ("ctx", "fsdp"), axis=0, tiled=True),
        lax.all_gather(down_weight, ("ctx", "fsdp"), axis=0, tiled=True),
    )
    tokens = hidden_in.shape[1]
    length = bucket_index.shape[0]
    head_count = bias_table.shape[1]
    buckets = bias_table.shape[0]
    query_first = lax.axis_index("ctx") * tokens
    bucket_rev = jnp.flip(jnp.concatenate([jnp.full((length,), -1, jnp.int32), bucket_index]))
    start_x = hidden_in[0].astype(jnp.float32)
    norm_one, normed_one, inverse_one = norm_forward(start_x, self_gain)
    query = product(norm_one, self_query).astype(jnp.bfloat16)
    keys_local = product(norm_one, self_key).astype(jnp.bfloat16)
    values_local = product(norm_one, self_value).astype(jnp.bfloat16)
    empty_top = jnp.full((head_count, tokens), NEGATIVE, jnp.float32)
    empty_total = jnp.zeros((head_count, tokens), jnp.float32)
    empty_mixed = jnp.zeros((tokens, head_count, query.shape[1] // head_count), jnp.float32)
    forward_bound = partial(
        forward_step,
        query=query,
        query_first=query_first,
        bucket_rev=bucket_rev,
        bias_table=bias_table,
    )
    top, total, mixed = fold_blocks(
        forward_bound,
        (empty_top, empty_total, empty_mixed),
        (
            lax.all_gather(keys_local, "ctx", axis=0, tiled=True),
            lax.all_gather(values_local, "ctx", axis=0, tiled=True),
        ),
        jnp.int32(0),
    )
    attn = (mixed / total.T[:, :, None]).reshape(tokens, -1).astype(jnp.bfloat16)
    self_lse = (top + jnp.log(total)).T
    after_self = start_x + product(attn, self_output)
    norm_two, normed_two, inverse_two = norm_forward(after_self, cross_gain)
    cross_q = product(norm_two, cross_query).astype(jnp.bfloat16)
    encoder_local = encoder_states[0]
    cross_k_local = product(encoder_local, cross_key).astype(jnp.bfloat16)
    cross_v_local = product(encoder_local, cross_value).astype(jnp.bfloat16)
    cross_keys, cross_values = (
        lax.all_gather(cross_k_local, "ctx", axis=0, tiled=True),
        lax.all_gather(cross_v_local, "ctx", axis=0, tiled=True),
    )
    cattn, cross_lse = plain_forward(cross_q, cross_keys, cross_values, head_count)
    after_cross = after_self + product(cattn, cross_output)
    norm_three, normed_three, inverse_three = norm_forward(after_cross, feed_gain)
    gate_pre = product(norm_three, gate_weight)
    linear_pre = product(norm_three, linear_weight)
    middle = geglu(gate_pre, linear_pre).astype(jnp.bfloat16)
    layer_out = (after_cross + product(middle, down_weight)).astype(jnp.bfloat16)
    grad_top = out_grad[0]
    grad_down = row_contract(middle, grad_top)
    grad_middle = col_contract(grad_top, down_weight)
    _, pull_back = jax.vjp(geglu, gate_pre, linear_pre)
    grad_gate_pre, grad_linear_pre = pull_back(grad_middle)
    gate_round = grad_gate_pre.astype(jnp.bfloat16)
    linear_round = grad_linear_pre.astype(jnp.bfloat16)
    grad_gate = row_contract(norm_three, gate_round)
    grad_linear = row_contract(norm_three, linear_round)
    back_three, grad_feed_gain = norm_backward(
        col_contract(gate_round, gate_weight) + col_contract(linear_round, linear_weight),
        normed_three,
        inverse_three,
        feed_gain,
    )
    grad_after_cross = grad_top.astype(jnp.float32) + back_three
    cross_round = grad_after_cross.astype(jnp.bfloat16)
    grad_cross_output = row_contract(cattn, cross_round)
    grad_cattn = col_contract(cross_round, cross_output).astype(jnp.bfloat16)
    grad_cq, cross_key_terms, cross_value_terms = plain_backward(
        cross_q, cross_keys, cross_values, cross_lse, cattn, grad_cattn, head_count
    )
    cross_key_sum, cross_value_sum = (
        lax.psum_scatter(
            cross_key_terms.astype(jnp.bfloat16), "ctx", scatter_dimension=0, tiled=True
        ).astype(jnp.float32),
        lax.psum_scatter(
            cross_value_terms.astype(jnp.bfloat16), "ctx", scatter_dimension=0, tiled=True
        ).astype(jnp.float32),
    )
    grad_cq = grad_cq.astype(jnp.bfloat16)
    cross_key_round = cross_key_sum.astype(jnp.bfloat16)
    cross_value_round = cross_value_sum.astype(jnp.bfloat16)
    grad_cross_query = row_contract(norm_two, grad_cq)
    grad_cross_key = row_contract(encoder_local, cross_key_round)
    grad_cross_value = row_contract(encoder_local, cross_value_round)
    encoder_grad = col_contract(cross_key_round, cross_key) + col_contract(
        cross_value_round, cross_value
    )
    back_two, grad_cross_gain = norm_backward(
        col_contract(grad_cq, cross_query), normed_two, inverse_two, cross_gain
    )
    grad_after_self = grad_after_cross + back_two
    self_round = grad_after_self.astype(jnp.bfloat16)
    grad_self_output = row_contract(attn, self_round)
    grad_attn = col_contract(self_round, self_output).astype(jnp.bfloat16)
    delta_rows = jnp.sum(
        by_heads(grad_attn, head_count).astype(jnp.float32)
        * by_heads(attn, head_count).astype(jnp.float32),
        axis=-1,
    )
    empty_rows = jnp.zeros((tokens, query.shape[1]), jnp.float32)
    empty_table = jnp.zeros((buckets, head_count), jnp.float32)
    partial_bound = partial(
        partial_step,
        query=query,
        grad_attn=grad_attn,
        lse_rows=self_lse,
        delta_rows=delta_rows,
        query_first=query_first,
        bucket_rev=bucket_rev,
        bias_table=bias_table,
    )
    empty_whole = jnp.zeros((length, query.shape[1]), jnp.float32)
    grad_query, key_terms, value_terms, table_part = fold_blocks(
        partial_bound,
        (empty_rows.reshape(tokens, head_count, -1), empty_whole, empty_whole, empty_table),
        (
            lax.all_gather(keys_local, "ctx", axis=0, tiled=True),
            lax.all_gather(values_local, "ctx", axis=0, tiled=True),
        ),
        jnp.int32(0),
    )
    key_sum, value_sum = (
        lax.psum_scatter(
            key_terms.astype(jnp.bfloat16), "ctx", scatter_dimension=0, tiled=True
        ).astype(jnp.float32),
        lax.psum_scatter(
            value_terms.astype(jnp.bfloat16), "ctx", scatter_dimension=0, tiled=True
        ).astype(jnp.float32),
    )
    grad_q = grad_query.reshape(tokens, -1).astype(jnp.bfloat16)
    grad_k = key_sum.astype(jnp.bfloat16)
    grad_v = value_sum.astype(jnp.bfloat16)
    grad_self_query = row_contract(norm_one, grad_q)
    grad_self_key = row_contract(norm_one, grad_k)
    grad_self_value = row_contract(norm_one, grad_v)
    upstream_one = (
        col_contract(grad_q, self_query)
        + col_contract(grad_k, self_key)
        + col_contract(grad_v, self_value)
    )
    back_one, grad_self_gain = norm_backward(upstream_one, normed_one, inverse_one, self_gain)
    input_grad = grad_after_self + back_one
    grad_table = lax.psum(table_part, ("seq", "ctx", "fsdp"))
    shard_grads = (
        lax.psum_scatter(grad_self_gain, ("ctx", "fsdp"), scatter_dimension=0, tiled=True),
        lax.psum_scatter(grad_self_query, ("ctx", "fsdp"), scatter_dimension=0, tiled=True),
        lax.psum_scatter(grad_self_key, ("ctx", "fsdp"), scatter_dimension=0, tiled=True),
        lax.psum_scatter(grad_self_value, ("ctx", "fsdp"), scatter_dimension=0, tiled=True),
        lax.psum_scatter(grad_self_output, ("ctx", "fsdp"), scatter_dimension=0, tiled=True),
        lax.psum_scatter(grad_cross_gain, ("ctx", "fsdp"), scatter_dimension=0, tiled=True),
        lax.psum_scatter(grad_cross_query, ("ctx", "fsdp"), scatter_dimension=0, tiled=True),
        lax.psum_scatter(grad_cross_key, ("ctx", "fsdp"), scatter_dimension=0, tiled=True),
        lax.psum_scatter(grad_cross_value, ("ctx", "fsdp"), scatter_dimension=0, tiled=True),
        lax.psum_scatter(grad_cross_output, ("ctx", "fsdp"), scatter_dimension=0, tiled=True),
        lax.psum_scatter(grad_feed_gain, ("ctx", "fsdp"), scatter_dimension=0, tiled=True),
        lax.psum_scatter(grad_gate, ("ctx", "fsdp"), scatter_dimension=0, tiled=True),
        lax.psum_scatter(grad_linear, ("ctx", "fsdp"), scatter_dimension=0, tiled=True),
        lax.psum_scatter(grad_down, ("ctx", "fsdp"), scatter_dimension=0, tiled=True),
    )
    summed = (
        lax.psum(shard_grads[0].astype(jnp.bfloat16), "seq").astype(jnp.float32),
        lax.psum(shard_grads[1].astype(jnp.bfloat16), "seq").astype(jnp.float32),
        lax.psum(shard_grads[2].astype(jnp.bfloat16), "seq").astype(jnp.float32),
        lax.psum(shard_grads[3].astype(jnp.bfloat16), "seq").astype(jnp.float32),
        lax.psum(shard_grads[4].astype(jnp.bfloat16), "seq").astype(jnp.float32),
        lax.psum(shard_grads[5].astype(jnp.bfloat16), "seq").astype(jnp.float32),
        lax.psum(shard_grads[6].astype(jnp.bfloat16), "seq").astype(jnp.float32),
        lax.psum(shard_grads[7].astype(jnp.bfloat16), "seq").astype(jnp.float32),
        lax.psum(shard_grads[8].astype(jnp.bfloat16), "seq").astype(jnp.float32),
        lax.psum(shard_grads[9].astype(jnp.bfloat16), "seq").astype(jnp.float32),
        lax.psum(shard_grads[10].astype(jnp.bfloat16), "seq").astype(jnp.float32),
        lax.psum(shard_grads[11].astype(jnp.bfloat16), "seq").astype(jnp.float32),
        lax.psum(shard_grads[12].astype(jnp.bfloat16), "seq").astype(jnp.float32),
        lax.psum(shard_grads[13].astype(jnp.bfloat16), "seq").astype(jnp.float32),
    )
    return (
        layer_out[None],
        input_grad[None],
        encoder_grad[None],
        grad_table,
        summed[0],
        summed[1],
        summed[2],
        summed[3],
        summed[4],
        summed[5],
        summed[6],
        summed[7],
        summed[8],
        summed[9],
        summed[10],
        summed[11],
        summed[12],
        summed[13],
    )


def solution(mesh):
    return jax.shard_map(
        per_device,
        mesh=mesh,
        in_specs=(
            P(("seq", "fsdp"), "ctx", None),
            P(("seq", "fsdp"), "ctx", None),
            P(("seq", "fsdp"), "ctx", None),
            P(),
            P(),
            P(("ctx", "fsdp")),
            P(("ctx", "fsdp"), None),
            P(("ctx", "fsdp"), None),
            P(("ctx", "fsdp"), None),
            P(("ctx", "fsdp"), None),
            P(("ctx", "fsdp")),
            P(("ctx", "fsdp"), None),
            P(("ctx", "fsdp"), None),
            P(("ctx", "fsdp"), None),
            P(("ctx", "fsdp"), None),
            P(("ctx", "fsdp")),
            P(("ctx", "fsdp"), None),
            P(("ctx", "fsdp"), None),
            P(("ctx", "fsdp"), None),
        ),
        out_specs=(
            P(("seq", "fsdp"), "ctx", None),
            P(("seq", "fsdp"), "ctx", None),
            P(("seq", "fsdp"), "ctx", None),
            P(),
            P(("ctx", "fsdp")),
            P(("ctx", "fsdp"), None),
            P(("ctx", "fsdp"), None),
            P(("ctx", "fsdp"), None),
            P(("ctx", "fsdp"), None),
            P(("ctx", "fsdp")),
            P(("ctx", "fsdp"), None),
            P(("ctx", "fsdp"), None),
            P(("ctx", "fsdp"), None),
            P(("ctx", "fsdp"), None),
            P(("ctx", "fsdp")),
            P(("ctx", "fsdp"), None),
            P(("ctx", "fsdp"), None),
            P(("ctx", "fsdp"), None),
        ),
        check_vma=False,
    )
```

profile of v0, /device:TPU:0, one launch (start us, length us, event | category | flops | bytes accessed | tf_op | source)
XLA Modules:
  0.0 1665.0 jit_solution(11337070283409407794)
XLA Ops:
  16.2 3.0 copy.90
  21.9 7.0 reshape.214
  30.9 24.1 %all-reduce.10 = (bf16[768]{0:T(1024)(128)(2,1)S(1)}, bf16[768]{0:T(1024)(128)(2,1)S(1)}, bf16[768]{0:T(1024)(128)(2,1)S(1)}) all-reduce(bf16[768]{0:T(1024)(128)(2,1)S(1)} %dynamic-update-slice, bf16[768]{0:T(1024)(128)(2,1)S(1)} %dynamic-update-slice.1, ...), channel_id=1, replica_groups=mesh['seq'=4,'ctx'=4,'fsdp'=2] {'ctx','fsdp'}, use_global_device_ids=true, to_apply=%add.3 | all-reduce | flops 2304 | bytes 9216
  57.0 21.0 %all_gather.59 = bf16[512,768]{1,0:T(8,128)(2,1)S(1)} all-gather(bf16[128,768]{1,0:T(8,128)(2,1)S(1)} %convolution_convert_fusion.9), channel_id=1, replica_groups=mesh['seq'=4,'ctx'=4,'fsdp'=2] {'ctx'}, dimensions={0}, use_global_device_ids=true | all-gather | bytes 983040 | tf_op jit(solution)/shard_map/all_gather | solution.py:349
  79.1 19.0 %all-gather.12.cloned.1.call-done = bf16[768,768]{1,0:T(8,128)(2,1)} async-done(((bf16[96,768]{1,0:T(8,128)(2,1)}), bf16[768,768]{1,0:T(8,128)(2,1)}) %all-gather.12.cloned.1.call-update) | async-done | bytes 1179664 | tf_op jit(solution)/shard_map/all_gather | solution.py:310
  100.6 39.6 %all-gather.16.cloned.1.call-done = bf16[768,768]{1,0:T(8,128)(2,1)} async-done(((bf16[96,768]{1,0:T(8,128)(2,1)}), bf16[768,768]{1,0:T(8,128)(2,1)}) %all-gather.16.cloned.1.call-update) | async-done | bytes 1179664 | tf_op jit(solution)/shard_map/all_gather | solution.py:312
  141.8 21.0 %all_gather.61 = bf16[512,768]{1,0:T(8,128)(2,1)S(1)} all-gather(bf16[128,768]{1,0:T(8,128)(2,1)S(1)} %convolution_convert_fusion.8), channel_id=1, replica_groups=mesh['seq'=4,'ctx'=4,'fsdp'=2] {'ctx'}, dimensions={0}, use_global_device_ids=true | all-gather | bytes 983040 | tf_op jit(solution)/shard_map/all_gather | solution.py:350
  163.9 3.0 fusion.104
  170.0 13.3 all-gather.18.cloned.1.call-done
  185.8 39.4 %all-gather.22.cloned.1.call-done = bf16[768,768]{1,0:T(8,128)(2,1)} async-done(((bf16[96,768]{1,0:T(8,128)(2,1)}), bf16[768,768]{1,0:T(8,128)(2,1)}) %all-gather.22.cloned.1.call-update) | async-done | bytes 1179664 | tf_op jit(solution)/shard_map/all_gather | solution.py:315
  229.4 37.7 %all-gather.24.cloned.1.call-done = bf16[768,768]{1,0:T(8,128)(2,1)} async-done(((bf16[96,768]{1,0:T(8,128)(2,1)}), bf16[768,768]{1,0:T(8,128)(2,1)}) %all-gather.24.cloned.1.call-update) | async-done | bytes 1179664 | tf_op jit(solution)/shard_map/all_gather | solution.py:316
  268.6 13.5 all_gather.68
  282.9 26.2 %all-gather.20.cloned.1.call-done = bf16[768,768]{1,0:T(8,128)(2,1)} async-done(((bf16[96,768]{1,0:T(8,128)(2,1)}), bf16[768,768]{1,0:T(8,128)(2,1)}) %all-gather.20.cloned.1.call-update) | async-done | bytes 1179664 | tf_op jit(solution)/shard_map/all_gather | solution.py:317
  310.7 13.5 all_gather.64
  329.0 22.2 %all-gather.26.cloned.1.call-done = bf16[768,768]{1,0:T(8,128)(2,1)} async-done(((bf16[96,768]{1,0:T(8,128)(2,1)}), bf16[768,768]{1,0:T(8,128)(2,1)}) %all-gather.26.cloned.1.call-update) | async-done | bytes 1179664 | tf_op jit(solution)/shard_map/all_gather | solution.py:318
  354.6 57.5 %all-gather.28.cloned.1.call-done = bf16[768,2048]{1,0:T(8,128)(2,1)} async-done(((bf16[96,2048]{1,0:T(8,128)(2,1)}), bf16[768,2048]{1,0:T(8,128)(2,1)}) %all-gather.28.cloned.1.call-update) | async-done | bytes 3145744 | tf_op jit(solution)/shard_map/all_gather | solution.py:320
  412.1 3.6 fusion.106
  415.7 57.2 %all-gather.30.cloned.1.call-done = bf16[768,2048]{1,0:T(8,128)(2,1)} async-done(((bf16[96,2048]{1,0:T(8,128)(2,1)}), bf16[768,2048]{1,0:T(8,128)(2,1)}) %all-gather.30.cloned.1.call-update) | async-done | bytes 3145744 | tf_op jit(solution)/shard_map/all_gather | solution.py:321
  472.9 3.6 fusion.107
  476.5 57.3 %all-gather.32.cloned.1.call-done = bf16[2048,768]{1,0:T(8,128)(2,1)} async-done(((bf16[256,768]{1,0:T(8,128)(2,1)}), bf16[2048,768]{1,0:T(8,128)(2,1)}) %all-gather.32.cloned.1.call-update) | async-done | bytes 3145744 | tf_op jit(solution)/shard_map/all_gather | solution.py:322
  533.8 5.0 multiply_convert_fusion
  569.6 3.3 subtract_multiply_fusion
  576.5 3.0 fusion.95
  579.6 3.0 fusion.85
  582.7 2.9 fusion.82
  592.9 3.1 copy.87
  598.7 3.0 copy.85
  601.9 16.3 reduce-scatter.48.cloned.1.call-done
  621.1 22.5 %reduce-scatter.46.cloned.1.call-done = bf16[128,768]{1,0:T(8,128)(2,1)} async-done(((bf16[512,768]{1,0:T(8,128)(2,1)}), bf16[128,768]{1,0:T(8,128)(2,1)}) %reduce-scatter.46.cloned.1.call-update) | async-done | bytes 196624
  646.6 4.8 fusion.111
  651.5 4.8 fusion.112
  656.3 4.7 fusion.70
  664.4 6.1 reshape.221
  675.3 39.7 %psum.105 = f32[32,12]{0,1:T(8,128)} all-reduce(f32[32,12]{0,1:T(8,128)S(1)} %fusion.64), channel_id=1, replica_groups=mesh['seq'=4,'ctx'=4,'fsdp'=2] {'seq','ctx','fsdp'}, use_global_device_ids=true, to_apply=%region_17.18 | all-reduce | flops 384 | bytes 3072 | tf_op jit(solution)/shard_map/psum | solution.py:467
  715.6 3.3 fusion.34
  721.0 67.6 %reduce-scatter.38.cloned.1.call-done = f32[96,768]{1,0:T(8,128)} async-done(((f32[768,768]{1,0:T(8,128)}), f32[96,768]{1,0:T(8,128)}) %reduce-scatter.38.cloned.1.call-update) | async-done | bytes 294928 | tf_op jit(solution)/shard_map/reduce_scatter | solution.py:478
  790.2 70.6 %reduce-scatter.34.cloned.1.call-done = f32[96,768]{1,0:T(8,128)} async-done(((f32[768,768]{1,0:T(8,128)}), f32[96,768]{1,0:T(8,128)}) %reduce-scatter.34.cloned.1.call-update) | async-done | bytes 294928 | tf_op jit(solution)/shard_map/reduce_scatter | solution.py:473
  862.5 70.9 %reduce-scatter.28.cloned.1.call-done = f32[96,768]{1,0:T(8,128)} async-done(((f32[768,768]{1,0:T(8,128)}), f32[96,768]{1,0:T(8,128)}) %reduce-scatter.28.cloned.1.call-update) | async-done | bytes 294928 | tf_op jit(solution)/shard_map/reduce_scatter | solution.py:470
  935.0 70.6 %reduce-scatter.56.cloned.1.call-done = f32[96,768]{1,0:T(8,128)} async-done(((f32[768,768]{1,0:T(8,128)}), f32[96,768]{1,0:T(8,128)}) %reduce-scatter.56.cloned.1.call-update) | async-done | bytes 294928
  1007.4 70.6 %reduce-scatter.54.cloned.1.call-done = f32[96,768]{1,0:T(8,128)} async-done(((f32[768,768]{1,0:T(8,128)}), f32[96,768]{1,0:T(8,128)}) %reduce-scatter.54.cloned.1.call-update) | async-done | bytes 294928
  1079.8 70.5 %reduce-scatter.32.cloned.1.call-done = f32[96,768]{1,0:T(8,128)} async-done(((f32[768,768]{1,0:T(8,128)}), f32[96,768]{1,0:T(8,128)}) %reduce-scatter.32.cloned.1.call-update) | async-done | bytes 294928 | tf_op jit(solution)/shard_map/reduce_scatter | solution.py:472
  1152.0 70.7 %reduce-scatter.30.cloned.1.call-done = f32[96,768]{1,0:T(8,128)} async-done(((f32[768,768]{1,0:T(8,128)}), f32[96,768]{1,0:T(8,128)}) %reduce-scatter.30.cloned.1.call-update) | async-done | bytes 294928 | tf_op jit(solution)/shard_map/reduce_scatter | solution.py:471
  1224.3 119.0 %reduce-scatter.40.cloned.1.call-done = f32[96,2048]{1,0:T(8,128)} async-done(((f32[768,2048]{1,0:T(8,128)}), f32[96,2048]{1,0:T(8,128)}) %reduce-scatter.40.cloned.1.call-update) | async-done | bytes 786448 | tf_op jit(solution)/shard_map/reduce_scatter | solution.py:480
  1345.2 119.0 %reduce-scatter.42.cloned.1.call-done = f32[96,2048]{1,0:T(8,128)} async-done(((f32[768,2048]{1,0:T(8,128)}), f32[96,2048]{1,0:T(8,128)}) %reduce-scatter.42.cloned.1.call-update) | async-done | bytes 786448 | tf_op jit(solution)/shard_map/reduce_scatter | solution.py:481
  1466.1 118.8 %reduce-scatter.44.cloned.1.call-done = f32[256,768]{1,0:T(8,128)} async-done(((f32[2048,768]{1,0:T(8,128)}), f32[256,768]{1,0:T(8,128)}) %reduce-scatter.44.cloned.1.call-update) | async-done | bytes 786448 | tf_op jit(solution)/shard_map/reduce_scatter | solution.py:482
  1591.6 35.4 %all-reduce.9 = (bf16[768]{0:T(1024)(128)(2,1)S(1)}, bf16[768]{0:T(1024)(128)(2,1)S(1)}, bf16[768]{0:T(1024)(128)(2,1)S(1)}) all-reduce(f32[768]{0:T(1024)S(1)} %get-tuple-element.76, f32[768]{0:T(1024)S(1)} %get-tuple-element.74, f32[768]{0:T(1024)S(1)} %get-tuple-element.72), channel_id=6, replica_groups=mesh['seq'=4,'ctx'=4,'fsdp'=2] {'ctx','fsdp'}, use_global_device_ids=true, to_apply=%region_19.20.clone | all-reduce | flops 2304 | bytes 13824
  1627.2 6.5 all-reduce.11
  1636.2 10.4 all-reduce.15.cloned.1.call-done
  (284 shorter events, 139.5 us)
Async XLA Ops:
  7.2 259.9 %copy-start = (bf16[1,16,768]{2,1,0:T(8,128)(2,1)S(1)}, bf16[1,16,768]{2,1,0:T(8,128)(2,1)}, u32[]{:S(2)}) copy-start(bf16[1,16,768]{2,1,0:T(8,128)(2,1)} %param.20) | copy-start | bytes 73732
  7.2 7.6 copy-start.49
  7.2 7.9 copy-start.50
  7.2 48.1 %all-gather.14.cloned.1.call-start = ((), (), s32[]{:S(2)}) async-start(), calls=%async_computation.16 | async-start | bytes 1327104 | tf_op jit(solution)/shard_map/all_gather | solution.py:311
  8.0 90.1 %all-gather.12.cloned.1.call-start = ((), (), s32[]{:S(2)}) async-start(), calls=%async_computation.15 | async-start | bytes 1327104 | tf_op jit(solution)/shard_map/all_gather | solution.py:310
  8.7 131.4 %all-gather.16.cloned.1.call-start = ((), (), s32[]{:S(2)}) async-start(), calls=%async_computation.17 | async-start | bytes 1327104 | tf_op jit(solution)/shard_map/all_gather | solution.py:312
  9.4 173.9 %all-gather.18.cloned.1.call-start = ((), (), s32[]{:S(2)}) async-start(), calls=%async_computation.18 | async-start | bytes 1327104 | tf_op jit(solution)/shard_map/all_gather | solution.py:313
  10.0 215.2 %all-gather.22.cloned.1.call-start = ((), (), s32[]{:S(2)}) async-start(), calls=%async_computation.20 | async-start | bytes 1327104 | tf_op jit(solution)/shard_map/all_gather | solution.py:315
  10.6 256.5 %all-gather.24.cloned.1.call-start = ((), (), s32[]{:S(2)}) async-start(), calls=%async_computation.21 | async-start | bytes 1327104 | tf_op jit(solution)/shard_map/all_gather | solution.py:316
  11.2 298.0 %all-gather.20.cloned.1.call-start = ((), (), s32[]{:S(2)}) async-start(), calls=%async_computation.19 | async-start | bytes 1327104 | tf_op jit(solution)/shard_map/all_gather | solution.py:317
  11.9 339.3 %all-gather.26.cloned.1.call-start = ((), (), s32[]{:S(2)}) async-start(), calls=%async_computation.22 | async-start | bytes 1327104 | tf_op jit(solution)/shard_map/all_gather | solution.py:318
  12.7 399.4 %all-gather.28.cloned.1.call-start = ((), (), s32[]{:S(2)}) async-start(), calls=%async_computation.23 | async-start | bytes 3538944 | tf_op jit(solution)/shard_map/all_gather | solution.py:320
  13.4 459.4 %all-gather.30.cloned.1.call-start = ((), (), s32[]{:S(2)}) async-start(), calls=%async_computation.24 | async-start | bytes 3538944 | tf_op jit(solution)/shard_map/all_gather | solution.py:321
  14.0 519.8 %all-gather.32.cloned.1.call-start = ((), (), s32[]{:S(2)}) async-start(), calls=%async_computation.25 | async-start | bytes 3538944 | tf_op jit(solution)/shard_map/all_gather | solution.py:322
  14.7 575.5 %reduce-scatter.52.cloned.1.call-start = ((), (), s32[]{:S(2)}) async-start(), calls=%async_computation.38 | async-start | bytes 122880
  21.9 7.0 copy-start.48
  21.9 8.3 copy-start.51
  21.9 8.5 copy-start.52
  21.9 8.8 copy-start.53
  21.9 33.1 %copy-start.3 = (bf16[1,128,768]{2,1,0:T(8,128)(2,1)S(1)}, bf16[1,128,768]{2,1,0:T(8,128)(2,1)}, u32[]{:S(2)}) copy-start(bf16[1,128,768]{2,1,0:T(8,128)(2,1)} %param.19) | copy-start | bytes 589828
  166.9 397.6 %copy-start.2 = (f32[12,128,512]{2,1,0:T(8,128)}, f32[12,128,512]{2,1,0:T(8,128)S(1)}, u32[]{:S(2)}) copy-start(f32[12,128,512]{2,1,0:T(8,128)S(1)} %get-tuple-element.106) | copy-start | bytes 9437188
  185.8 81.3 %copy-start.44 = (f32[128]{0:T(128)}, f32[128]{0:T(128)S(1)}, u32[]{:S(2)}) copy-start(f32[128]{0:T(128)S(1)} %add_rsqrt_fusion.1) | copy-start | bytes 1540
  543.3 9.7 copy-start.45
  556.0 40.0 %reduce-scatter.50.cloned.1.call-start = ((), (), s32[]{:S(2)}) async-start(), calls=%async_computation.37 | async-start | bytes 122880
  564.2 54.0 %reduce-scatter.48.cloned.1.call-start = ((), (), s32[]{:S(2)}) async-start(), calls=%async_computation.36 | async-start | bytes 983040
  569.4 74.2 %reduce-scatter.46.cloned.1.call-start = ((), (), s32[]{:S(2)}) async-start(), calls=%async_computation.35 | async-start | bytes 983040
  576.5 142.8 %reduce-scatter.36.cloned.1.call-start = ((), (), s32[]{:S(2)}) async-start(), calls=%async_computation.30 | async-start | bytes 2654208 | tf_op jit(solution)/shard_map/reduce_scatter | solution.py:475
  579.6 209.0 %reduce-scatter.38.cloned.1.call-start = ((), (), s32[]{:S(2)}) async-start(), calls=%async_computation.31 | async-start | bytes 2654208 | tf_op jit(solution)/shard_map/reduce_scatter | solution.py:478
  582.6 278.2 %reduce-scatter.34.cloned.1.call-start = ((), (), s32[]{:S(2)}) async-start(), calls=%async_computation.29 | async-start | bytes 2654208 | tf_op jit(solution)/shard_map/reduce_scatter | solution.py:473
  585.6 347.7 %reduce-scatter.28.cloned.1.call-start = ((), (), s32[]{:S(2)}) async-start(), calls=%async_computation.26 | async-start | bytes 2654208 | tf_op jit(solution)/shard_map/reduce_scatter | solution.py:470
  590.2 415.4 %reduce-scatter.56.cloned.1.call-start = ((), (), s32[]{:S(2)}) async-start(), calls=%async_computation.40 | async-start | bytes 2654208
  596.0 482.0 %reduce-scatter.54.cloned.1.call-start = ((), (), s32[]{:S(2)}) async-start(), calls=%async_computation.39 | async-start | bytes 2654208
  601.8 548.5 %reduce-scatter.32.cloned.1.call-start = ((), (), s32[]{:S(2)}) async-start(), calls=%async_computation.28 | async-start | bytes 2654208 | tf_op jit(solution)/shard_map/reduce_scatter | solution.py:472
  621.1 601.6 %reduce-scatter.30.cloned.1.call-start = ((), (), s32[]{:S(2)}) async-start(), calls=%async_computation.27 | async-start | bytes 2654208 | tf_op jit(solution)/shard_map/reduce_scatter | solution.py:471
  646.5 696.8 %reduce-scatter.40.cloned.1.call-start = ((), (), s32[]{:S(2)}) async-start(), calls=%async_computation.32 | async-start | bytes 7077888 | tf_op jit(solution)/shard_map/reduce_scatter | solution.py:480
  651.4 812.8 %reduce-scatter.42.cloned.1.call-start = ((), (), s32[]{:S(2)}) async-start(), calls=%async_computation.33 | async-start | bytes 7077888 | tf_op jit(solution)/shard_map/reduce_scatter | solution.py:481
  656.3 928.7 %reduce-scatter.44.cloned.1.call-start = ((), (), s32[]{:S(2)}) async-start(), calls=%async_computation.34 | async-start | bytes 7077888 | tf_op jit(solution)/shard_map/reduce_scatter | solution.py:482
  661.1 985.5 %all-reduce.15.cloned.1.call-start = ((), (), s32[]{:S(2)}) async-start(), calls=%async_computation.41 | async-start | bytes 4915200 | tf_op jit(solution)/shard_map/psum | solution.py:492
  674.3 40.7 %copy-start.16 = (bf16[768,768]{1,0:T(8,128)(2,1)S(1)}, bf16[768,768]{1,0:T(8,128)(2,1)}, u32[]{:S(2)}) copy-start(bf16[768,768]{1,0:T(8,128)(2,1)} %all-gather.12.cloned.1.call-done) | copy-start | bytes 3538948
  674.4 40.7 %copy-start.26 = (bf16[12,64,128]{2,1,0:T(8,128)(2,1)S(1)}, bf16[12,64,128]{2,1,0:T(8,128)(2,1)}, u32[]{:S(2)}) copy-start(bf16[12,64,128]{2,1,0:T(8,128)(2,1)} %copy-done.25) | copy-start | bytes 589828
  674.4 41.2 %copy-start.9 = (f32[128,768]{1,0:T(8,128)S(1)}, f32[128,768]{1,0:T(8,128)}, u32[]{:S(2)}) copy-start(f32[128,768]{1,0:T(8,128)} %copy-done.7) | copy-start | bytes 1179652
  674.4 41.2 %copy-start.20 = (bf16[128,2048]{1,0:T(8,128)(2,1)S(1)}, bf16[128,2048]{1,0:T(8,128)(2,1)}, u32[]{:S(2)}) copy-start(bf16[128,2048]{1,0:T(8,128)(2,1)} %get-tuple-element.100) | copy-start | bytes 1572868
  1345.2 241.7 %copy-start.42 = (bf16[16,768]{1,0:T(8,128)(2,1)S(1)}, bf16[16,768]{1,0:T(8,128)(2,1)}, u32[]{:S(2)}) copy-start(bf16[16,768]{1,0:T(8,128)(2,1)} %reduce-scatter.52.cloned.1.call-done) | copy-start | bytes 73732
  1466.1 123.3 %copy-start.14 = (bf16[768,768]{1,0:T(8,128)(2,1)S(1)}, bf16[768,768]{1,0:T(8,128)(2,1)}, u32[]{:S(2)}) copy-start(bf16[768,768]{1,0:T(8,128)(2,1)} %all-gather.14.cloned.1.call-done) | copy-start | bytes 3538948
  1589.4 45.8 %copy-start.12 = (f32[128,768]{1,0:T(8,128)S(1)}, f32[128,768]{1,0:T(8,128)}, u32[]{:S(2)}) copy-start(f32[128,768]{1,0:T(8,128)} %copy-done.11) | copy-start | bytes 1179652
  1646.6 7.2 copy-start.38
  1648.6 7.4 copy-start.35
  1650.6 7.1 copy-start.1
  (33 other events, 111.8 us)
Sparse Core Ops, SparseCore 0:
  10.2 44.3 all-gather.13
  56.8 41.2 all-gather.11
  100.3 39.7 all-gather.15
  142.2 41.1 all-gather.17
  185.4 39.8 all-gather.21
  227.2 39.7 all-gather.23
  269.3 39.8 all-gather.19
  311.3 39.8 all-gather.25
  353.4 58.6 all-gather.27
  414.1 58.6 all-gather.29
  475.0 58.6 all-gather.31
  556.1 18.0 reduce-scatter.51
  577.1 17.5 reduce-scatter.49
  596.8 21.3 reduce-scatter.47
  620.9 22.6 reduce-scatter.45
  646.9 69.2 reduce-scatter.35
  719.6 68.9 reduce-scatter.37
  792.0 68.8 reduce-scatter.33
  864.3 68.9 reduce-scatter.27
  936.7 68.8 reduce-scatter.55
  1009.1 68.8 reduce-scatter.53
  1081.5 68.7 reduce-scatter.31
  1153.8 68.7 reduce-scatter.29
  1226.1 117.1 reduce-scatter.39
  1346.9 117.2 reduce-scatter.41
  1467.6 117.2 reduce-scatter.43
  1589.7 56.8 all-reduce.14
where the time goes:
time: 1680 us; the launch traced here: 1670 us
  waiting for transfers between devices  1270 us (76%)
  blocking collectives  175 us (10%)
  matrix products  102 us (6%)
  local copies, waits for them, and re-layouts  62.7 us (4%)
  other arithmetic  32.8 us (2%)
  between operations  16.9 us (1%)
    unnamed x33, waiting for transfers between devices  187 us
    reduce_scatter x1, waiting for transfers between devices, per_device(): lax.psum_scatter(grad_gate, ('ctx', 'fsdp'), scatter_dimension=0, tiled=T...  119 us
    reduce_scatter x1, waiting for transfers between devices, per_device(): lax.psum_scatter(grad_linear, ('ctx', 'fsdp'), scatter_dimension=0, tiled...  119 us
    reduce_scatter x1, waiting for transfers between devices, per_device(): lax.psum_scatter(grad_down, ('ctx', 'fsdp'), scatter_dimension=0, tiled=T...  119 us
    reduce_scatter x1, waiting for transfers between devices, per_device(): lax.psum_scatter(grad_self_query, ('ctx', 'fsdp'), scatter_dimension=0, t...  70.9 us
    reduce_scatter x1, waiting for transfers between devices, per_device(): lax.psum_scatter(grad_self_key, ('ctx', 'fsdp'), scatter_dimension=0, til...  70.7 us
    reduce_scatter x1, waiting for transfers between devices, per_device(): lax.psum_scatter(grad_self_output, ('ctx', 'fsdp'), scatter_dimension=0,...  70.6 us
    reduce_scatter x1, waiting for transfers between devices, per_device(): lax.psum_scatter(grad_self_value, ('ctx', 'fsdp'), scatter_dimension=0, t...  70.5 us
  transfers between devices with their start and end apart: 27, of which 23 were waited for; matrix products, arithmetic and copies ran while one was open for 10% of the time, Pallas kernels for 0%

commit v1 on v0

--- a/solution.py
+++ b/solution.py
@@ -9,6 +9,34 @@
 EPSILON = 1e-06
 NEGATIVE = -1e30
 HIGHEST = lax.Precision.HIGHEST
+
+
+LANES = 128
+
+
+def fold_rows(rows, height):
+    count = -(-rows.shape[-2] // height)
+    short = count * height - rows.shape[-2]
+    padding = [(0, 0)] * (rows.ndim - 2) + [(0, short), (0, 0)]
+    padded = jnp.pad(rows, padding)
+    return jnp.concatenate(
+        [padded[..., number * height : (number + 1) * height, :] for number in range(count)],
+        axis=-1,
+    )
+
+
+def unfold_rows(columns, row_count, features):
+    count = columns.shape[-1] // features
+    stacked = jnp.concatenate(
+        [columns[..., number * features : (number + 1) * features] for number in range(count)],
+        axis=-2,
+    )
+    return stacked[..., :row_count, :]
+
+
+def gain_columns(gains, dtype):
+    columns = jnp.stack([member.astype(dtype) for member in gains], axis=1)
+    return jnp.pad(columns, ((0, 0), (0, LANES - columns.shape[1])))
 
 
 def product(left, right):
@@ -269,6 +297,33 @@
     return (grad_query, grad_keys, grad_values)
 
 
+def reduce_terms(terms):
+    groups = lax.axis_size("seq")
+    share = terms.shape[1] // groups
+    stacked = jnp.stack(
+        [terms[:, number * share : (number + 1) * share] for number in range(groups)]
+    )
+    part = lax.psum_scatter(stacked, "seq", scatter_dimension=0, tiled=False)
+    part = lax.psum_scatter(part, ("ctx", "fsdp"), scatter_dimension=0, tiled=True)
+    return join_columns(lax.all_gather(part, "seq", axis=0, tiled=False))
+
+
+def join_columns(stacked):
+    return jnp.concatenate([stacked[number] for number in range(stacked.shape[0])], axis=1)
+
+
+def gather_pack(pack):
+    share = pack.shape[1] // lax.axis_size("seq")
+    own = lax.dynamic_slice_in_dim(pack, lax.axis_index("seq") * share, share, 1)
+    rows = lax.all_gather(own, ("ctx", "fsdp"), axis=0, tiled=True)
+    return join_columns(lax.all_gather(rows, "seq", axis=0, tiled=False))
+
+
+def even_columns(members):
+    joined = jnp.concatenate(members, axis=1)
+    return jnp.pad(joined, ((0, 0), (0, -joined.shape[1] % (LANES * lax.axis_size("seq")))))
+
+
 def per_device(
     hidden_in,
     encoder_states,
@@ -290,37 +345,46 @@
     linear_weight,
     down_weight,
 ):
+    shards = lax.axis_size(("ctx", "fsdp"))
+    features = self_query.shape[1]
+    hidden = gate_weight.shape[1]
+    pack = even_columns(
+        [
+            self_query,
+            self_key,
+            self_value,
+            self_output,
+            cross_query,
+            cross_key,
+            cross_value,
+            cross_output,
+            gate_weight,
+            linear_weight,
+            fold_rows(down_weight, self_query.shape[0]),
+            gain_columns((self_gain, cross_gain, feed_gain), jnp.bfloat16),
+        ]
+    )
+    pack = gather_pack(pack)
     (
-        self_gain,
         self_query,
         self_key,
         self_value,
         self_output,
-        cross_gain,
         cross_query,
         cross_key,
         cross_value,
         cross_output,
-        feed_gain,
-        gate_weight,
-        linear_weight,
-        down_weight,
-    ) = (
-        lax.all_gather(self_gain, ("ctx", "fsdp"), axis=0, tiled=True),
-        lax.all_gather(self_query, ("ctx", "fsdp"), axis=0, tiled=True),
-        lax.all_gather(self_key, ("ctx", "fsdp"), axis=0, tiled=True),
-        lax.all_gather(self_value, ("ctx", "fsdp"), axis=0, tiled=True),
-        lax.all_gather(self_output, ("ctx", "fsdp"), axis=0, tiled=True),
-        lax.all_gather(cross_gain, ("ctx", "fsdp"), axis=0, tiled=True),
-        lax.all_gather(cross_query, ("ctx", "fsdp"), axis=0, tiled=True),
-        lax.all_gather(cross_key, ("ctx", "fsdp"), axis=0, tiled=True),
-        lax.all_gather(cross_value, ("ctx", "fsdp"), axis=0, tiled=True),
-        lax.all_gather(cross_output, ("ctx", "fsdp"), axis=0, tiled=True),
-        lax.all_gather(feed_gain, ("ctx", "fsdp"), axis=0, tiled=True),
-        lax.all_gather(gate_weight, ("ctx", "fsdp"), axis=0, tiled=True),
-        lax.all_gather(linear_weight, ("ctx", "fsdp"), axis=0, tiled=True),
-        lax.all_gather(down_weight, ("ctx", "fsdp"), axis=0, tiled=True),
-    )
+    ) = (pack[:, number * features : (number + 1) * features] for number in range(8))
+    first = 8 * features
+    gate_weight = pack[:, first : first + hidden]
+    linear_weight = pack[:, first + hidden : first + 2 * hidden]
+    first = first + 2 * hidden
+    width = -(-(hidden // shards) // (features // shards)) * features
+    down_weight = unfold_rows(
+        pack[:, first : first + width].reshape(shards, -1, width), hidden // shards, features
+    ).reshape(hidden, features)
+    gains = pack[:, first + width : first + width + LANES].T
+    self_gain, cross_gain, feed_gain = gains[0], gains[1], gains[2]
     tokens = hidden_in.shape[1]
     length = bucket_index.shape[0]
     head_count = bias_table.shape[1]
@@ -329,9 +393,18 @@
     bucket_rev = jnp.flip(jnp.concatenate([jnp.full((length,), -1, jnp.int32), bucket_index]))
     start_x = hidden_in[0].astype(jnp.float32)
     norm_one, normed_one, inverse_one = norm_forward(start_x, self_gain)
-    query = product(norm_one, self_query).astype(jnp.bfloat16)
-    keys_local = product(norm_one, self_key).astype(jnp.bfloat16)
-    values_local = product(norm_one, self_value).astype(jnp.bfloat16)
+    projected = product(norm_one, pack[:, : 3 * features]).astype(jnp.bfloat16)
+    query = projected[:, :features]
+    encoder_local = encoder_states[0]
+    cross_local = product(encoder_local, pack[:, 5 * features : 7 * features]).astype(jnp.bfloat16)
+    encoder_rows = encoder_local.shape[0]
+    blocks = lax.all_gather(
+        jnp.concatenate([projected[:, features:], cross_local], axis=0), "ctx", axis=0, tiled=False
+    )
+    both = blocks[:, :tokens].reshape(length, 2 * features)
+    keys, values = both[:, :features], both[:, features:]
+    both = blocks[:, tokens:].reshape(-1, 2 * features)
+    cross_keys, cross_values = both[:, :features], both[:, features:]
     empty_top = jnp.full((head_count, tokens), NEGATIVE, jnp.float32)
     empty_total = jnp.zeros((head_count, tokens), jnp.float32)
     empty_mixed = jnp.zeros((tokens, head_count, query.shape[1] // head_count), jnp.float32)
@@ -345,10 +418,7 @@
     top, total, mixed = fold_blocks(
         forward_bound,
         (empty_top, empty_total, empty_mixed),
-        (
-            lax.all_gather(keys_local, "ctx", axis=0, tiled=True),
-            lax.all_gather(values_local, "ctx", axis=0, tiled=True),
-        ),
+        (keys, values),
         jnp.int32(0),
     )
     attn = (mixed / total.T[:, :, None]).reshape(tokens, -1).astype(jnp.bfloat16)
@@ -356,13 +426,6 @@
     after_self = start_x + product(attn, self_output)
     norm_two, normed_two, inverse_two = norm_forward(after_self, cross_gain)
     cross_q = product(norm_two, cross_query).astype(jnp.bfloat16)
-    encoder_local = encoder_states[0]
-    cross_k_local = product(encoder_local, cross_key).astype(jnp.bfloat16)
-    cross_v_local = product(encoder_local, cross_value).astype(jnp.bfloat16)
-    cross_keys, cross_values = (
-        lax.all_gather(cross_k_local, "ctx", axis=0, tiled=True),
-        lax.all_gather(cross_v_local, "ctx", axis=0, tiled=True),
-    )
     cattn, cross_lse = plain_forward(cross_q, cross_keys, cross_values, head_count)
     after_cross = after_self + product(cattn, cross_output)
     norm_three, normed_three, inverse_three = norm_forward(after_cross, feed_gain)
@@ -392,23 +455,8 @@
     grad_cq, cross_key_terms, cross_value_terms = plain_backward(
         cross_q, cross_keys, cross_values, cross_lse, cattn, grad_cattn, head_count
     )
-    cross_key_sum, cross_value_sum = (
-        lax.psum_scatter(
-            cross_key_terms.astype(jnp.bfloat16), "ctx", scatter_dimension=0, tiled=True
-        ).astype(jnp.float32),
-        lax.psum_scatter(
-            cross_value_terms.astype(jnp.bfloat16), "ctx", scatter_dimension=0, tiled=True
-        ).astype(jnp.float32),
-    )
     grad_cq = grad_cq.astype(jnp.bfloat16)
-    cross_key_round = cross_key_sum.astype(jnp.bfloat16)
-    cross_value_round = cross_value_sum.astype(jnp.bfloat16)
     grad_cross_query = row_contract(norm_two, grad_cq)
-    grad_cross_key = row_contract(encoder_local, cross_key_round)
-    grad_cross_value = row_contract(encoder_local, cross_value_round)
-    encoder_grad = col_contract(cross_key_round, cross_key) + col_contract(
-        cross_value_round, cross_value
-    )
     back_two, grad_cross_gain = norm_backward(
         col_contract(grad_cq, cross_query), normed_two, inverse_two, cross_gain
     )
@@ -437,85 +485,70 @@
     grad_query, key_terms, value_terms, table_part = fold_blocks(
         partial_bound,
         (empty_rows.reshape(tokens, head_count, -1), empty_whole, empty_whole, empty_table),
-        (
-            lax.all_gather(keys_local, "ctx", axis=0, tiled=True),
-            lax.all_gather(values_local, "ctx", axis=0, tiled=True),
-        ),
+        (keys, values),
         jnp.int32(0),
     )
-    key_sum, value_sum = (
-        lax.psum_scatter(
-            key_terms.astype(jnp.bfloat16), "ctx", scatter_dimension=0, tiled=True
-        ).astype(jnp.float32),
-        lax.psum_scatter(
-            value_terms.astype(jnp.bfloat16), "ctx", scatter_dimension=0, tiled=True
-        ).astype(jnp.float32),
-    )
+    terms = jnp.concatenate(
+        [
+            jnp.concatenate([key_terms, value_terms], axis=1).reshape(-1, tokens, 2 * features),
+            jnp.concatenate([cross_key_terms, cross_value_terms], axis=1).reshape(
+                -1, encoder_rows, 2 * features
+            ),
+        ],
+        axis=1,
+    ).astype(jnp.bfloat16)
+    sums = lax.psum_scatter(terms, "ctx", scatter_dimension=0, tiled=False)
+    cross_both = sums[tokens:]
+    grad_cross_both = row_contract(encoder_local, cross_both)
+    grad_cross_key, grad_cross_value = (
+        grad_cross_both[:, :features],
+        grad_cross_both[:, features:],
+    )
+    encoder_grad = col_contract(cross_both, pack[:, 5 * features : 7 * features])
     grad_q = grad_query.reshape(tokens, -1).astype(jnp.bfloat16)
-    grad_k = key_sum.astype(jnp.bfloat16)
-    grad_v = value_sum.astype(jnp.bfloat16)
-    grad_self_query = row_contract(norm_one, grad_q)
-    grad_self_key = row_contract(norm_one, grad_k)
-    grad_self_value = row_contract(norm_one, grad_v)
-    upstream_one = (
-        col_contract(grad_q, self_query)
-        + col_contract(grad_k, self_key)
-        + col_contract(grad_v, self_value)
-    )
+    grad_projected = jnp.concatenate([grad_q, sums[:tokens]], axis=1)
+    grad_self_projections = row_contract(norm_one, grad_projected)
+    upstream_one = col_contract(grad_projected, pack[:, : 3 * features])
     back_one, grad_self_gain = norm_backward(upstream_one, normed_one, inverse_one, self_gain)
     input_grad = grad_after_self + back_one
     grad_table = lax.psum(table_part, ("seq", "ctx", "fsdp"))
-    shard_grads = (
-        lax.psum_scatter(grad_self_gain, ("ctx", "fsdp"), scatter_dimension=0, tiled=True),
-        lax.psum_scatter(grad_self_query, ("ctx", "fsdp"), scatter_dimension=0, tiled=True),
-        lax.psum_scatter(grad_self_key, ("ctx", "fsdp"), scatter_dimension=0, tiled=True),
-        lax.psum_scatter(grad_self_value, ("ctx", "fsdp"), scatter_dimension=0, tiled=True),
-        lax.psum_scatter(grad_self_output, ("ctx", "fsdp"), scatter_dimension=0, tiled=True),
-        lax.psum_scatter(grad_cross_gain, ("ctx", "fsdp"), scatter_dimension=0, tiled=True),
-        lax.psum_scatter(grad_cross_query, ("ctx", "fsdp"), scatter_dimension=0, tiled=True),
-        lax.psum_scatter(grad_cross_key, ("ctx", "fsdp"), scatter_dimension=0, tiled=True),
-        lax.psum_scatter(grad_cross_value, ("ctx", "fsdp"), scatter_dimension=0, tiled=True),
-        lax.psum_scatter(grad_cross_output, ("ctx", "fsdp"), scatter_dimension=0, tiled=True),
-        lax.psum_scatter(grad_feed_gain, ("ctx", "fsdp"), scatter_dimension=0, tiled=True),
-        lax.psum_scatter(grad_gate, ("ctx", "fsdp"), scatter_dimension=0, tiled=True),
-        lax.psum_scatter(grad_linear, ("ctx", "fsdp"), scatter_dimension=0, tiled=True),
-        lax.psum_scatter(grad_down, ("ctx", "fsdp"), scatter_dimension=0, tiled=True),
-    )
-    summed = (
-        lax.psum(shard_grads[0].astype(jnp.bfloat16), "seq").astype(jnp.float32),
-        lax.psum(shard_grads[1].astype(jnp.bfloat16), "seq").astype(jnp.float32),
-        lax.psum(shard_grads[2].astype(jnp.bfloat16), "seq").astype(jnp.float32),
-        lax.psum(shard_grads[3].astype(jnp.bfloat16), "seq").astype(jnp.float32),
-        lax.psum(shard_grads[4].astype(jnp.bfloat16), "seq").astype(jnp.float32),
-        lax.psum(shard_grads[5].astype(jnp.bfloat16), "seq").astype(jnp.float32),
-        lax.psum(shard_grads[6].astype(jnp.bfloat16), "seq").astype(jnp.float32),
-        lax.psum(shard_grads[7].astype(jnp.bfloat16), "seq").astype(jnp.float32),
-        lax.psum(shard_grads[8].astype(jnp.bfloat16), "seq").astype(jnp.float32),
-        lax.psum(shard_grads[9].astype(jnp.bfloat16), "seq").astype(jnp.float32),
-        lax.psum(shard_grads[10].astype(jnp.bfloat16), "seq").astype(jnp.float32),
-        lax.psum(shard_grads[11].astype(jnp.bfloat16), "seq").astype(jnp.float32),
-        lax.psum(shard_grads[12].astype(jnp.bfloat16), "seq").astype(jnp.float32),
-        lax.psum(shard_grads[13].astype(jnp.bfloat16), "seq").astype(jnp.float32),
-    )
+    folded = fold_rows(grad_down.reshape(shards, -1, features), features // shards)
+    parts = [
+        grad_self_projections,
+        grad_self_output,
+        grad_cross_query,
+        grad_cross_both,
+        grad_cross_output,
+        grad_gate,
+        grad_linear,
+        folded.reshape(features, width),
+        gain_columns((grad_self_gain, grad_cross_gain, grad_feed_gain), jnp.bfloat16),
+    ]
+    terms = even_columns([member.astype(jnp.bfloat16) for member in parts])
+    summed = reduce_terms(terms).astype(jnp.float32)
+    squares = [summed[:, number * features : (number + 1) * features] for number in range(8)]
+    first = 8 * features
+    down_first = first + 2 * hidden
+    gain_first = down_first + width
     return (
         layer_out[None],
         input_grad[None],
         encoder_grad[None],
         grad_table,
-        summed[0],
-        summed[1],
-        summed[2],
-        summed[3],
-        summed[4],
-        summed[5],
-        summed[6],
-        summed[7],
-        summed[8],
-        summed[9],
-        summed[10],
-        summed[11],
-        summed[12],
-        summed[13],
+        summed[:, gain_first],
+        squares[0],
+        squares[1],
+        squares[2],
+        squares[3],
+        summed[:, gain_first + 1],
+        squares[4],
+        squares[5],
+        squares[6],
+        squares[7],
+        summed[:, gain_first + 2],
+        summed[:, first : first + hidden],
+        summed[:, first + hidden : down_first],
+        unfold_rows(summed[:, down_first:gain_first], hidden // shards, features),
     )
 
 

time: 1680 us -> 786 us (0.47)
  waiting for transfers between devices: 1270 us -> 486 us
  blocking collectives: 175 us -> 40.8 us
  local copies, waits for them, and re-layouts: 62.7 us -> 99.2 us
  matrix products: 102 us -> 81.3 us
    reduce_scatter x9 -> x3, waiting for transfers between devices: 707 us -> 271 us  [the longest x1 142 us: reduce_terms(): part = lax.psum_scatter(stacked, 'seq', scatter_dimension=0, tiled=False)]
    unnamed x33 -> x7, waiting for transfers between devices: 187 us -> 0.11 us
    all_gather x11 -> x4, waiting for transfers between devices: 369 us -> 216 us  [the longest x1 108 us: gather_pack(): return join_columns(lax.all_gather(rows, 'seq', axis=0, tiled=False))]
    all_gather x4 -> x0, blocking collectives: 68.9 us -> none  [the longest x1 21 us: per_device(): lax.all_gather(keys_local, 'ctx', axis=0, tiled=True)]
    unnamed x2 -> x0, blocking collectives: 59.5 us -> none
    convert_element_type x24 -> x1, other arithmetic: 26.5 us -> 0.88 us  [per_device(): summed = reduce_terms(terms).astype(jnp.float32)]
    slice x0 -> x14, local copies, waits for them, and re-layouts: none -> 21.9 us  [the longest x2 9.62 us: join_columns(): stacked[number]]
    another operation x0 -> x4, other arithmetic: none -> 19.1 us  [the longest x2 19.1 us: reduce_terms(): jnp.stack([terms[:, number * share:(number + 1) * share] for number in ra...]
  transfers between devices with their start and end apart: 27 -> 7, of which waited for: 23 -> 6; matrix products, arithmetic and copies ran while one was open for 10% -> 8% of each run, Pallas kernels for 0% -> 0%
where the time goes in v1:
time: 786 us; the launch traced here: 781 us
  waiting for transfers between devices  486 us (62%)
  local copies, waits for them, and re-layouts  99.2 us (13%)
  matrix products  81.3 us (10%)
  other arithmetic  45.9 us (6%)
  blocking collectives  40.8 us (5%)
  between operations  27.1 us (3%)
    reduce_scatter x1, waiting for transfers between devices, reduce_terms(): part = lax.psum_scatter(stacked, 'seq', scatter_dimension=0, tiled=False)  142 us
    all_gather x1, waiting for transfers between devices, gather_pack(): return join_columns(lax.all_gather(rows, 'seq', axis=0, tiled=False))  108 us
    reduce_scatter x1, waiting for transfers between devices, reduce_terms(): lax.psum_scatter(part, ('ctx', 'fsdp'), scatter_dimension=0, tiled=True)  102 us
    all_gather x1, waiting for transfers between devices, gather_pack(): rows = lax.all_gather(own, ('ctx', 'fsdp'), axis=0, tiled=True)  84.6 us
    psum x1, blocking collectives, per_device(): grad_table = lax.psum(table_part, ('seq', 'ctx', 'fsdp'))  40.8 us
    reduce_scatter x1, waiting for transfers between devices, per_device(): sums = lax.psum_scatter(terms, 'ctx', scatter_dimension=0, tiled=False)  26.7 us
    unnamed x128, local copies, waits for them, and re-layouts  25.5 us
    dot_general x8, matrix products, row_contract(): lax.dot_general(left, right, (((0,), (0,)), ((), ())), preferred_element_...  24.5 us
  transfers between devices with their start and end apart: 7, of which 6 were waited for; matrix products, arithmetic and copies ran while one was open for 8% of the time, Pallas kernels for 0%

profile of v1, /device:TPU:0, one launch (start us, length us, event | category | flops | bytes accessed | tf_op | source)
XLA Modules:
  0.0 781.1 jit_solution(10825351969024771895)
XLA Ops:
  17.1 84.6 %all-gather.8.cloned.1.call-done = bf16[768,3200]{1,0:T(8,128)(2,1)} async-done(((bf16[96,3200]{1,0:T(8,128)(2,1)}), bf16[768,3200]{1,0:T(8,128)(2,1)}) %all-gather.8.cloned.1.call-update) | async-done | bytes 4915216 | tf_op jit(solution)/shard_map/all_gather | solution.py:318
  103.7 3.0 copy.114
  106.8 3.1 slice.306
  109.9 7.5 reshape.250
  117.7 108.2 %all-gather.10.cloned.1.call-done = bf16[3072,3200]{1,0:T(8,128)(2,1)} async-done(((bf16[768,3200]{1,0:T(8,128)(2,1)}), bf16[3072,3200]{1,0:T(8,128)(2,1)}) %all-gather.10.cloned.1.call-update) | async-done | bytes 19660816 | tf_op jit(solution)/shard_map/all_gather | solution.py:319
  227.2 2.7 convolution_convert_fusion.1
  230.0 2.1 fusion.12
  233.8 2.2 slice.320
  236.0 7.8 %fusion.121 = (bf16[768,3200]{1,0:T(8,128)(2,1)S(1)}, bf16[768,3200]{1,0:T(8,128)(2,1)S(1)}, bf16[768,3200]{1,0:T(8,128)(2,1)S(1)}, bf16[768,3200]{1,0:T(8,128)(2,1)S(1)}) fusion(bf16[3072,3200]{1,0:T(8,128)(2,1)} %all-gather.10.cloned.1.call-done), kind=kLoop, calls=%fused_computation.239 | loop fusion | bytes 39321600 | tf_op jit(solution)/shard_map/slice | solution.py:312
  247.2 3.4 pad_maximum_fusion.11
  250.6 22.8 %all-gather.12.cloned.1.call-done = bf16[576,1536]{1,0:T(8,128)(2,1)} async-done(((bf16[144,1536]{1,0:T(8,128)(2,1)}), bf16[576,1536]{1,0:T(8,128)(2,1)}) %all-gather.12.cloned.1.call-update) | async-done | bytes 1769488 | tf_op jit(solution)/shard_map/all_gather | solution.py:401
  277.0 3.0 fusion.127
  284.1 2.3 copy.111
  290.6 2.0 fusion.47
  300.0 1.9 multiply_reduce_fusion.6
  310.2 2.5 convolution_convert_fusion.16
  315.6 2.0 fusion.51
  320.2 1.9 fusion.50
  332.8 2.5 convolution_convert_fusion.14
  350.5 2.6 fusion.29
  356.1 3.3 subtract_multiply_fusion
  360.7 2.4 concatenate.81
  363.1 2.2 copy.92
  365.3 2.8 maximum_maximum_fusion
  368.2 2.5 convolution_convert_fusion.13
  372.4 2.1 copy.109
  374.5 2.0 convolution_convert_fusion.5
  378.9 26.7 %reduce-scatter.4.cloned.1.call-done = bf16[1,144,1536]{2,1,0:T(8,128)(2,1)} async-done(((bf16[4,144,1536]{2,1,0:T(8,128)(2,1)}), bf16[1,144,1536]{2,1,0:T(8,128)(2,1)}) %reduce-scatter.4.cloned.1.call-update) | async-done | bytes 442384 | tf_op jit(solution)/shard_map/reduce_scatter | solution.py:500
  406.7 5.2 constant_dynamic-update-slice_fusion.18
  411.9 2.0 constant_dynamic-update-slice_fusion.17
  413.9 2.0 constant_dynamic-update-slice_fusion.16
  415.9 3.9 constant_dynamic-update-slice_fusion.15
  419.8 1.9 constant_dynamic-update-slice_fusion.14
  421.8 3.7 constant_dynamic-update-slice_fusion.13
  425.5 3.7 constant_dynamic-update-slice_fusion.12
  429.2 4.1 fusion.88
  433.5 4.2 constant_dynamic-update-slice_fusion.11
  438.4 2.8 fusion
  441.5 7.7 fusion.2
  449.2 11.4 %pad_maximum_fusion = bf16[4,768,3200]{2,1,0:T(8,128)(2,1)} fusion(bf16[1,768,3200]{2,1,0:T(8,128)(2,1)S(1)} %fusion, bf16[1,768,3200]{2,1,0:T(8,128)(2,1)S(1)} %get-tuple-element.40, bf16[1,768,3200]{2,1,0:T(8,128)(2,1)S(1)} %get-tuple-element.39, bf16[1,768,3200]{2,1,0:T(8,128)(2,1)} %get-tuple-element.65), kind=kLoop, calls=%fused_computation | loop fusion | flops 29491200 | bytes 39321600 | tf_op jit(solution)/shard_map/stack | solution.py:303
  460.7 141.5 %reduce-scatter.6.cloned.1.call-done = bf16[1,768,3200]{2,1,0:T(8,128)(2,1)} async-done(((bf16[4,768,3200]{2,1,0:T(8,128)(2,1)}), bf16[1,768,3200]{2,1,0:T(8,128)(2,1)}) %reduce-scatter.6.cloned.1.call-update) | async-done | bytes 4915216 | tf_op jit(solution)/shard_map/reduce_scatter | solution.py:306
  602.3 102.5 %reduce-scatter.8.cloned.1.call-done = bf16[96,3200]{1,0:T(8,128)(2,1)} async-done(((bf16[768,3200]{1,0:T(8,128)(2,1)}), bf16[96,3200]{1,0:T(8,128)(2,1)}) %reduce-scatter.8.cloned.1.call-update) | async-done | bytes 614416 | tf_op jit(solution)/shard_map/reduce_scatter | solution.py:307
  704.8 2.4 pad.37
  707.1 6.0 reshape.260
  713.2 3.2 pad.38
  718.4 40.8 %psum.7 = f32[32,12]{0,1:T(8,128)} all-reduce(f32[32,12]{0,1:T(8,128)S(1)} %fusion.93), channel_id=1, replica_groups=mesh['seq'=4,'ctx'=4,'fsdp'=2] {'seq','ctx','fsdp'}, use_global_device_ids=true, to_apply=%region_14.15 | all-reduce | flops 384 | bytes 3072 | tf_op jit(solution)/shard_map/psum | solution.py:514
  759.3 3.2 fusion.52
  762.5 3.0 fusion.53
  (227 shorter events, 86.3 us)
Async XLA Ops:
  7.2 222.8 %copy-start = (bf16[1,16,768]{2,1,0:T(8,128)(2,1)S(1)}, bf16[1,16,768]{2,1,0:T(8,128)(2,1)}, u32[]{:S(2)}) copy-start(bf16[1,16,768]{2,1,0:T(8,128)(2,1)} %param.20) | copy-start | bytes 73732
  7.2 8.6 %copy-start.40 = (bf16[96,2048]{1,0:T(8,128)(2,1)S(1)}, bf16[96,2048]{1,0:T(8,128)(2,1)}, u32[]{:S(2)}) copy-start(bf16[96,2048]{1,0:T(8,128)(2,1)} %param.36) | copy-start | bytes 1179652
  7.2 8.6 %copy-start.37 = (bf16[256,768]{1,0:T(8,128)(2,1)S(1)}, bf16[256,768]{1,0:T(8,128)(2,1)}, u32[]{:S(2)}) copy-start(bf16[256,768]{1,0:T(8,128)(2,1)} %param.37) | copy-start | bytes 1179652
  7.2 8.7 %copy-start.50 = (bf16[96]{0:T(256)(128)(2,1)S(1)}, bf16[96]{0:T(256)(128)(2,1)}, u32[]{:S(2)}) copy-start(bf16[96]{0:T(256)(128)(2,1)} %param.34) | copy-start | bytes 580
  7.2 8.7 %copy-start.51 = (bf16[96]{0:T(256)(128)(2,1)S(1)}, bf16[96]{0:T(256)(128)(2,1)}, u32[]{:S(2)}) copy-start(bf16[96]{0:T(256)(128)(2,1)} %param.29) | copy-start | bytes 580
  7.2 8.7 %copy-start.52 = (bf16[96]{0:T(256)(128)(2,1)S(1)}, bf16[96]{0:T(256)(128)(2,1)}, u32[]{:S(2)}) copy-start(bf16[96]{0:T(256)(128)(2,1)} %param.24) | copy-start | bytes 580
  7.3 94.4 %all-gather.8.cloned.1.call-start = ((), (), s32[]{:S(2)}) async-start(), calls=%async_computation.3 | async-start | bytes 5529600 | tf_op jit(solution)/shard_map/all_gather | solution.py:318
  17.0 84.8 %copy-start.49 = (s32[512]{0:T(512)S(1)}, s32[512]{0:T(512)}, u32[]{:S(2)}) copy-start(s32[512]{0:T(512)} %param.22) | copy-start | bytes 6148
  17.0 85.7 %copy-start.53 = (f32[32,12]{0,1:T(8,128)S(1)}, f32[32,12]{0,1:T(8,128)}, u32[]{:S(2)}) copy-start(f32[32,12]{0,1:T(8,128)} %param.23) | copy-start | bytes 4612
  17.0 208.9 %all-gather.10.cloned.1.call-start = ((), (), s32[]{:S(2)}) async-start(), calls=%async_computation.7 | async-start | bytes 24576000 | tf_op jit(solution)/shard_map/all_gather | solution.py:319
  101.7 171.6 %all-gather.12.cloned.1.call-start = ((), (), s32[]{:S(2)}) async-start(), calls=%async_computation.8 | async-start | bytes 2211840 | tf_op jit(solution)/shard_map/all_gather | solution.py:401
  109.9 7.5 copy-start.22
  117.6 112.4 %copy-start.47 = (f32[128]{0:T(128)}, f32[128]{0:T(128)S(1)}, u32[]{:S(2)}) copy-start(f32[128]{0:T(128)S(1)} %add_rsqrt_fusion.2) | copy-start | bytes 1540
  232.9 172.7 %reduce-scatter.4.cloned.1.call-start = ((), (), s32[]{:S(2)}) async-start(), calls=%async_computation.4 | async-start | bytes 2211840 | tf_op jit(solution)/shard_map/reduce_scatter | solution.py:500
  279.9 70.5 %copy-start.2 = (f32[12,128,512]{2,1,0:T(8,128)}, f32[12,128,512]{2,1,0:T(8,128)S(1)}, u32[]{:S(2)}) copy-start(f32[12,128,512]{2,1,0:T(8,128)S(1)} %get-tuple-element.71) | copy-start | bytes 9437188
  290.6 4.6 copy-start.10
  294.4 27.7 %copy-start.43 = (f32[128]{0:T(128)}, f32[128]{0:T(128)S(1)}, u32[]{:S(2)}) copy-start(f32[128]{0:T(128)S(1)} %add_rsqrt_fusion.1) | copy-start | bytes 1540
  297.3 4.7 copy-start.36
  297.3 4.8 copy-start.4
  300.0 2.8 copy-start.3
  302.0 7.3 copy-start.12
  302.7 4.0 copy-start.13
  306.7 2.5 copy-start.25
  306.7 2.5 copy-start.27
  314.4 7.8 copy-start.6
  314.4 7.8 copy-start.11
  320.2 3.2 copy-start.34
  356.1 3.3 copy-start.29
  368.1 234.1 %reduce-scatter.6.cloned.1.call-start = ((), (), s32[]{:S(2)}) async-start(), calls=%async_computation.5 | async-start | bytes 24576000 | tf_op jit(solution)/shard_map/reduce_scatter | solution.py:306
  377.0 29.7 %copy-start.48 = (f32[128]{0:T(128)S(1)}, f32[128]{0:T(128)}, u32[]{:S(2)}) copy-start(f32[128]{0:T(128)} %copy-done.47) | copy-start | bytes 1540
  406.6 5.3 copy-start.17
  406.6 5.3 copy-start.31
  406.7 7.2 copy-start.35
  406.7 7.2 copy-start.44
  413.9 6.0 copy-start.20
  413.9 6.0 copy-start.33
  415.9 5.9 copy-start.28
  421.8 3.8 copy-start.26
  425.5 3.7 copy-start.23
  425.5 3.7 copy-start.39
  438.4 3.1 copy-start.14
  460.6 244.1 %reduce-scatter.8.cloned.1.call-start = ((), (), s32[]{:S(2)}) async-start(), calls=%async_computation.6 | async-start | bytes 5529600 | tf_op jit(solution)/shard_map/reduce_scatter | solution.py:307
  602.2 164.3 %all-gather.14.cloned.1.call-start = ((), (), s32[]{:S(2)}) async-start(), calls=%async_computation.9 | async-start | bytes 3072000 | tf_op jit(solution)/shard_map/all_gather | solution.py:308
  717.4 41.8 %copy-start.9 = (bf16[8,256,768]{2,1,0:T(8,128)(2,1)S(1)}, bf16[8,256,768]{2,1,0:T(8,128)(2,1)}, u32[]{:S(2)}) copy-start(bf16[8,256,768]{2,1,0:T(8,128)(2,1)} %pad_maximum_fusion.8) | copy-start | bytes 9437188
  759.3 6.3 copy-start.18
  759.3 6.3 copy-start.24
  759.3 6.3 copy-start.41
  770.8 3.2 copy-start.1
  (13 other events, 19.3 us)
Sparse Core Ops, SparseCore 0:
  17.1 84.4 all-gather.7
  103.2 122.6 all-gather.9
  233.0 40.2 all-gather.11
  368.2 37.3 reduce-scatter.3
  460.7 141.4 reduce-scatter.5
  605.8 98.9 reduce-scatter.7
  706.3 24.7 all-gather.13

commit v2 on v1

--- a/solution.py
+++ b/solution.py
@@ -297,15 +297,17 @@
     return (grad_query, grad_keys, grad_values)
 
 
-def reduce_terms(terms):
+def reduce_terms(terms, table_terms):
     groups = lax.axis_size("seq")
     share = terms.shape[1] // groups
     stacked = jnp.stack(
         [terms[:, number * share : (number + 1) * share] for number in range(groups)]
     )
     part = lax.psum_scatter(stacked, "seq", scatter_dimension=0, tiled=False)
+    table = lax.psum(table_terms, ("seq", "ctx", "fsdp"))
+    part, table = lax.optimization_barrier((part, table))
     part = lax.psum_scatter(part, ("ctx", "fsdp"), scatter_dimension=0, tiled=True)
-    return join_columns(lax.all_gather(part, "seq", axis=0, tiled=False))
+    return join_columns(lax.all_gather(part, "seq", axis=0, tiled=False)), table
 
 
 def join_columns(stacked):
@@ -511,7 +513,6 @@
     upstream_one = col_contract(grad_projected, pack[:, : 3 * features])
     back_one, grad_self_gain = norm_backward(upstream_one, normed_one, inverse_one, self_gain)
     input_grad = grad_after_self + back_one
-    grad_table = lax.psum(table_part, ("seq", "ctx", "fsdp"))
     folded = fold_rows(grad_down.reshape(shards, -1, features), features // shards)
     parts = [
         grad_self_projections,
@@ -525,7 +526,8 @@
         gain_columns((grad_self_gain, grad_cross_gain, grad_feed_gain), jnp.bfloat16),
     ]
     terms = even_columns([member.astype(jnp.bfloat16) for member in parts])
-    summed = reduce_terms(terms).astype(jnp.float32)
+    summed, grad_table = reduce_terms(terms, table_part)
+    summed = summed.astype(jnp.float32)
     squares = [summed[:, number * features : (number + 1) * features] for number in range(8)]
     first = 8 * features
     down_first = first + 2 * hidden

time: 786 us -> 753 us (0.958)
  waiting for transfers between devices: 486 us -> 452 us
  other arithmetic: 45.9 us -> 59 us
  between operations: 27.1 us -> 15.2 us
    reduce_scatter x1, waiting for transfers between devices: 142 us -> 87.4 us  [reduce_terms(): part = lax.psum_scatter(stacked, 'seq', scatter_dimension=0, tiled=False)]
    all_gather x1, waiting for transfers between devices: 0.01 us -> 18.5 us  [reduce_terms(): lax.all_gather(part, 'seq', axis=0, tiled=False)]
    reduce_sum x1, other arithmetic: 1.68 us -> 14.5 us  [per_device(): jnp.sum(by_heads(grad_attn, head_count).astype(jnp.float32) * by_heads(at...]
    unnamed x128 -> x122, local copies, waits for them, and re-layouts: 25.5 us -> 23.2 us
  transfers between devices with their start and end apart: 7 -> 7, of which waited for: 6 -> 7; matrix products, arithmetic and copies ran while one was open for 8% -> 9% of each run, Pallas kernels for 0% -> 0%
where the time goes in v2:
time: 753 us; the launch traced here: 749 us
  waiting for transfers between devices  452 us (60%)
  local copies, waits for them, and re-layouts  99.8 us (13%)
  matrix products  83.3 us (11%)
  other arithmetic  59 us (8%)
  blocking collectives  39.5 us (5%)
  between operations  15.2 us (2%)
    all_gather x1, waiting for transfers between devices, gather_pack(): return join_columns(lax.all_gather(rows, 'seq', axis=0, tiled=False))  108 us
    reduce_scatter x1, waiting for transfers between devices, reduce_terms(): lax.psum_scatter(part, ('ctx', 'fsdp'), scatter_dimension=0, tiled=True)  102 us
    reduce_scatter x1, waiting for transfers between devices, reduce_terms(): part = lax.psum_scatter(stacked, 'seq', scatter_dimension=0, tiled=False)  87.4 us
    all_gather x1, waiting for transfers between devices, gather_pack(): rows = lax.all_gather(own, ('ctx', 'fsdp'), axis=0, tiled=True)  84.6 us
    psum x1, blocking collectives, reduce_terms(): table = lax.psum(table_terms, ('seq', 'ctx', 'fsdp'))  39.5 us
    reduce_scatter x1, waiting for transfers between devices, per_device(): sums = lax.psum_scatter(terms, 'ctx', scatter_dimension=0, tiled=False)  26.8 us
    dot_general x8, matrix products, row_contract(): lax.dot_general(left, right, (((0,), (0,)), ((), ())), preferred_element_...  25.8 us
    all_gather x1, waiting for transfers between devices, per_device(): lax.all_gather(jnp.concatenate([projected[:, features:], cross_local], ax...  23.6 us
  transfers between devices with their start and end apart: 7, of which 7 were waited for; matrix products, arithmetic and copies ran while one was open for 9% of the time, Pallas kernels for 0%

profile of v2, /device:TPU:0, one launch (start us, length us, event | category | flops | bytes accessed | tf_op | source)
XLA Modules:
  0.0 748.8 jit_solution(6574467797897865814)
XLA Ops:
  17.7 84.6 %all-gather.8.cloned.1.call-done = bf16[768,3200]{1,0:T(8,128)(2,1)} async-done(((bf16[96,3200]{1,0:T(8,128)(2,1)}), bf16[768,3200]{1,0:T(8,128)(2,1)}) %all-gather.8.cloned.1.call-update) | async-done | bytes 4915216 | tf_op jit(solution)/shard_map/all_gather | solution.py:320
  104.4 3.0 copy.114
  107.4 3.2 slice.306
  110.6 7.5 %reshape.250 = f32[12,128,639]{2,1,0:T(8,128)} reshape(f32[12,81792]{1,0:T(8,128)} %slice.306) | data formatting | bytes 7852032 | tf_op jit(solution)/shard_map/reshape | solution.py:97
  118.3 108.2 %all-gather.10.cloned.1.call-done = bf16[3072,3200]{1,0:T(8,128)(2,1)} async-done(((bf16[768,3200]{1,0:T(8,128)(2,1)}), bf16[3072,3200]{1,0:T(8,128)(2,1)}) %all-gather.10.cloned.1.call-update) | async-done | bytes 19660816 | tf_op jit(solution)/shard_map/all_gather | solution.py:321
  227.9 2.7 convolution_convert_fusion.1
  231.4 2.1 fusion.12
  234.4 2.2 slice.320
  236.6 7.8 %fusion.121 = (bf16[768,3200]{1,0:T(8,128)(2,1)S(1)}, bf16[768,3200]{1,0:T(8,128)(2,1)S(1)}, bf16[768,3200]{1,0:T(8,128)(2,1)S(1)}, bf16[768,3200]{1,0:T(8,128)(2,1)S(1)}) fusion(bf16[3072,3200]{1,0:T(8,128)(2,1)} %all-gather.10.cloned.1.call-done), kind=kLoop, calls=%fused_computation.239 | loop fusion | bytes 39321600 | tf_op jit(solution)/shard_map/slice | solution.py:314
  247.8 3.4 pad_maximum_fusion.11
  251.2 23.6 %all-gather.12.cloned.1.call-done = bf16[576,1536]{1,0:T(8,128)(2,1)} async-done(((bf16[144,1536]{1,0:T(8,128)(2,1)}), bf16[576,1536]{1,0:T(8,128)(2,1)}) %all-gather.12.cloned.1.call-update) | async-done | bytes 1769488 | tf_op jit(solution)/shard_map/all_gather | solution.py:403
  280.0 3.0 fusion.127
  288.8 2.3 copy.111
  310.7 2.5 convolution_convert_fusion.16
  333.3 2.5 convolution_convert_fusion.14
  337.5 14.5 %multiply_reduce_fusion.2 = f32[128,12]{0,1:T(8,128)S(1)} fusion(bf16[128,12,64]{0,2,1:T(8,128)(2,1)} %copy-done.29, bf16[128,12,64]{0,2,1:T(8,128)(2,1)} %bitcast.193), kind=kLoop, calls=%fused_computation.143 | loop fusion | flops 391680 | bytes 399360 | tf_op jit(solution)/shard_map/reduce_sum | solution.py:469
  352.1 2.6 fusion.29
  354.7 2.6 subtract_multiply_fusion
  357.3 2.4 concatenate.82
  359.7 2.2 copy.93
  361.9 2.2 fusion.32
  364.1 2.4 concatenate.81
  366.5 2.2 copy.92
  368.7 2.8 maximum_maximum_fusion
  371.6 2.0 copy.109
  373.7 2.5 convolution_convert_fusion.13
  377.9 2.0 convolution_convert_fusion.5
  382.3 26.8 %reduce-scatter.4.cloned.1.call-done = bf16[1,144,1536]{2,1,0:T(8,128)(2,1)} async-done(((bf16[4,144,1536]{2,1,0:T(8,128)(2,1)}), bf16[1,144,1536]{2,1,0:T(8,128)(2,1)}) %reduce-scatter.4.cloned.1.call-update) | async-done | bytes 442384 | tf_op jit(solution)/shard_map/reduce_scatter | solution.py:502
  410.1 5.2 constant_dynamic-update-slice_fusion.18
  415.3 4.1 fusion.88
  420.2 3.1 constant_dynamic-update-slice_fusion.17
  423.3 3.1 constant_dynamic-update-slice_fusion.16
  426.3 3.1 constant_dynamic-update-slice_fusion.15
  431.4 3.7 constant_dynamic-update-slice_fusion.13
  435.1 3.7 constant_dynamic-update-slice_fusion.12
  438.8 2.2 constant_dynamic-update-slice_fusion.11
  441.8 2.7 fusion
  444.4 7.7 %fusion.2 = (bf16[1,768,3200]{2,1,0:T(8,128)(2,1)S(1)}, bf16[1,768,3200]{2,1,0:T(8,128)(2,1)S(1)}, bf16[1,768,3200]{2,1,0:T(8,128)(2,1)}) fusion(bf16[768,2048]{1,0:T(8,128)(2,1)} %get-tuple-element.96, bf16[768,768]{1,0:T(8,128)(2,1)} %get-tuple-element.94, bf16[768,1536]{1,0:T(8,128)(2,1)S(1)} %get-tuple-element.92, bf16[768,768]{1,0:T(8,128)(2,1)} %get-tuple-element.90, ...), kind=kLoop, calls=%fused_computation.7 | loop fusion | flops 44236800 | bytes 30474240 | tf_op jit(solution)/shard_map/stack | solution.py:303
  452.1 11.4 %pad_maximum_fusion = bf16[4,768,3200]{2,1,0:T(8,128)(2,1)} fusion(bf16[1,768,3200]{2,1,0:T(8,128)(2,1)S(1)} %fusion, bf16[1,768,3200]{2,1,0:T(8,128)(2,1)S(1)} %get-tuple-element.44, bf16[1,768,3200]{2,1,0:T(8,128)(2,1)S(1)} %get-tuple-element.43, bf16[1,768,3200]{2,1,0:T(8,128)(2,1)} %get-tuple-element.69), kind=kLoop, calls=%fused_computation | loop fusion | flops 29491200 | bytes 39321600 | tf_op jit(solution)/shard_map/stack | solution.py:303
  463.6 2.4 pad.40
  466.0 6.4 reshape.260
  472.4 4.5 pad.41
  479.0 39.5 %psum.7 = f32[32,12]{0,1:T(8,128)} all-reduce(f32[32,12]{0,1:T(8,128)S(1)} %fusion.93), channel_id=1, replica_groups=mesh['seq'=4,'ctx'=4,'fsdp'=2] {'seq','ctx','fsdp'}, use_global_device_ids=true, to_apply=%region_18.19 | all-reduce | flops 384 | bytes 3072 | tf_op jit(solution)/shard_map/psum | solution.py:307
  518.5 87.4 %reduce-scatter.6.cloned.1.call-done = bf16[1,768,3200]{2,1,0:T(8,128)(2,1)} async-done(((bf16[4,768,3200]{2,1,0:T(8,128)(2,1)}), bf16[1,768,3200]{2,1,0:T(8,128)(2,1)}) %reduce-scatter.6.cloned.1.call-update) | async-done | bytes 4915216 | tf_op jit(solution)/shard_map/reduce_scatter | solution.py:306
  605.9 102.4 %reduce-scatter.8.cloned.1.call-done = bf16[96,3200]{1,0:T(8,128)(2,1)} async-done(((bf16[768,3200]{1,0:T(8,128)(2,1)}), bf16[96,3200]{1,0:T(8,128)(2,1)}) %reduce-scatter.8.cloned.1.call-update) | async-done | bytes 614416 | tf_op jit(solution)/shard_map/reduce_scatter | solution.py:309
  708.5 3.2 fusion.52
  711.7 3.0 fusion.53
  715.7 18.5 %all-gather.14.cloned.1.call-done = bf16[384,3200]{1,0:T(8,128)(2,1)} async-done(((bf16[96,3200]{1,0:T(8,128)(2,1)}), bf16[384,3200]{1,0:T(8,128)(2,1)}) %all-gather.14.cloned.1.call-update) | async-done | bytes 2457616 | tf_op jit(solution)/shard_map/all_gather | solution.py:310
  (221 shorter events, 90.5 us)
Async XLA Ops:
  7.2 224.2 %copy-start = (bf16[1,16,768]{2,1,0:T(8,128)(2,1)S(1)}, bf16[1,16,768]{2,1,0:T(8,128)(2,1)}, u32[]{:S(2)}) copy-start(bf16[1,16,768]{2,1,0:T(8,128)(2,1)} %param.20) | copy-start | bytes 73732
  7.2 9.4 %copy-start.39 = (bf16[96,2048]{1,0:T(8,128)(2,1)S(1)}, bf16[96,2048]{1,0:T(8,128)(2,1)}, u32[]{:S(2)}) copy-start(bf16[96,2048]{1,0:T(8,128)(2,1)} %param.36) | copy-start | bytes 1179652
  7.2 9.4 %copy-start.34 = (bf16[256,768]{1,0:T(8,128)(2,1)S(1)}, bf16[256,768]{1,0:T(8,128)(2,1)}, u32[]{:S(2)}) copy-start(bf16[256,768]{1,0:T(8,128)(2,1)} %param.37) | copy-start | bytes 1179652
  7.2 95.1 %all-gather.8.cloned.1.call-start = ((), (), s32[]{:S(2)}) async-start(), calls=%async_computation.3 | async-start | bytes 5529600 | tf_op jit(solution)/shard_map/all_gather | solution.py:320
  17.6 84.8 %copy-start.49 = (s32[512]{0:T(512)S(1)}, s32[512]{0:T(512)}, u32[]{:S(2)}) copy-start(s32[512]{0:T(512)} %param.22) | copy-start | bytes 6148
  17.6 85.7 %copy-start.50 = (f32[32,12]{0,1:T(8,128)S(1)}, f32[32,12]{0,1:T(8,128)}, u32[]{:S(2)}) copy-start(f32[32,12]{0,1:T(8,128)} %param.23) | copy-start | bytes 4612
  17.6 208.9 %all-gather.10.cloned.1.call-start = ((), (), s32[]{:S(2)}) async-start(), calls=%async_computation.7 | async-start | bytes 24576000 | tf_op jit(solution)/shard_map/all_gather | solution.py:321
  102.3 172.4 %all-gather.12.cloned.1.call-start = ((), (), s32[]{:S(2)}) async-start(), calls=%async_computation.8 | async-start | bytes 2211840 | tf_op jit(solution)/shard_map/all_gather | solution.py:403
  110.6 7.5 %copy-start.22 = (bf16[1,128,768]{2,1,0:T(8,128)(2,1)S(1)}, bf16[1,128,768]{2,1,0:T(8,128)(2,1)}, u32[]{:S(2)}) copy-start(bf16[1,128,768]{2,1,0:T(8,128)(2,1)} %param.19) | copy-start | bytes 589828
  118.2 112.3 %copy-start.47 = (f32[128]{0:T(128)}, f32[128]{0:T(128)S(1)}, u32[]{:S(2)}) copy-start(f32[128]{0:T(128)S(1)} %add_rsqrt_fusion.2) | copy-start | bytes 1540
  234.3 174.7 %reduce-scatter.4.cloned.1.call-start = ((), (), s32[]{:S(2)}) async-start(), calls=%async_computation.4 | async-start | bytes 2211840 | tf_op jit(solution)/shard_map/reduce_scatter | solution.py:502
  283.0 69.1 %copy-start.1 = (f32[12,128,512]{2,1,0:T(8,128)}, f32[12,128,512]{2,1,0:T(8,128)S(1)}, u32[]{:S(2)}) copy-start(f32[12,128,512]{2,1,0:T(8,128)S(1)} %get-tuple-element.75) | copy-start | bytes 9437188
  283.0 2.6 copy-start.36
  291.1 4.6 copy-start.10
  294.9 27.7 %copy-start.43 = (f32[128]{0:T(128)}, f32[128]{0:T(128)S(1)}, u32[]{:S(2)}) copy-start(f32[128]{0:T(128)S(1)} %add_rsqrt_fusion.1) | copy-start | bytes 1540
  297.8 4.7 copy-start.33
  297.8 4.8 copy-start.3
  300.5 2.8 copy-start.2
  302.5 7.3 copy-start.12
  303.3 4.0 copy-start.13
  303.3 2.5 copy-start.8
  303.3 2.5 copy-start.37
  305.0 2.2 copy-start.19
  307.3 2.5 copy-start.25
  307.3 2.5 copy-start.27
  314.9 7.7 %copy-start.6 = (f32[128,768]{1,0:T(8,128)S(1)}, f32[128,768]{1,0:T(8,128)}, u32[]{:S(2)}) copy-start(f32[128,768]{1,0:T(8,128)} %copy-done.5) | copy-start | bytes 1179652
  314.9 7.7 %copy-start.11 = (bf16[768,768]{1,0:T(8,128)(2,1)S(1)}, bf16[768,768]{1,0:T(8,128)(2,1)}, u32[]{:S(2)}) copy-start(bf16[768,768]{1,0:T(8,128)(2,1)} %pad_maximum_fusion.12) | copy-start | bytes 3538948
  337.5 17.1 %copy-start.20 = (bf16[512,768]{0,1:T(8,128)(2,1)S(1)}, bf16[512,768]{0,1:T(8,128)(2,1)}, u32[]{:S(2)}) copy-start(bf16[512,768]{0,1:T(8,128)(2,1)} %copy.111) | copy-start | bytes 2359300
  337.5 17.1 %copy-start.21 = (bf16[128,768]{0,1:T(8,128)(2,1)S(1)}, bf16[128,768]{0,1:T(8,128)(2,1)}, u32[]{:S(2)}) copy-start(bf16[128,768]{0,1:T(8,128)(2,1)} %copy.91) | copy-start | bytes 589828
  368.7 4.9 copy-start.42
  371.6 234.3 %reduce-scatter.6.cloned.1.call-start = ((), (), s32[]{:S(2)}) async-start(), calls=%async_computation.5 | async-start | bytes 24576000 | tf_op jit(solution)/shard_map/reduce_scatter | solution.py:306
  380.4 29.7 %copy-start.48 = (f32[128]{0:T(128)S(1)}, f32[128]{0:T(128)}, u32[]{:S(2)}) copy-start(f32[128]{0:T(128)} %copy-done.47) | copy-start | bytes 1540
  410.1 5.2 copy-start.23
  410.1 5.2 copy-start.38
  419.3 3.9 copy-start.44
  420.2 3.1 copy-start.7
  423.3 6.2 copy-start.18
  423.3 6.2 copy-start.31
  426.3 5.1 copy-start.28
  431.4 3.7 copy-start.26
  435.1 3.7 copy-start.4
  438.8 2.2 copy-start.35
  463.6 244.8 %reduce-scatter.8.cloned.1.call-start = ((), (), s32[]{:S(2)}) async-start(), calls=%async_computation.6 | async-start | bytes 5529600 | tf_op jit(solution)/shard_map/reduce_scatter | solution.py:309
  478.7 229.7 %copy-start.9 = (bf16[8,256,768]{2,1,0:T(8,128)(2,1)S(1)}, bf16[8,256,768]{2,1,0:T(8,128)(2,1)}, u32[]{:S(2)}) copy-start(bf16[8,256,768]{2,1,0:T(8,128)(2,1)} %pad_maximum_fusion.8) | copy-start | bytes 9437188
  605.9 128.3 %all-gather.14.cloned.1.call-start = ((), (), s32[]{:S(2)}) async-start(), calls=%async_computation.9 | async-start | bytes 3072000 | tf_op jit(solution)/shard_map/all_gather | solution.py:310
  708.4 6.3 copy-start.16
  708.4 6.3 copy-start.24
  708.5 6.3 copy-start.40
  (10 other events, 12.1 us)
Sparse Core Ops, SparseCore 0:
  17.8 84.4 all-gather.7
  103.9 122.6 all-gather.9
  234.5 40.2 all-gather.11
  371.7 37.3 reduce-scatter.3
  463.7 142.1 reduce-scatter.5
  609.4 98.9 reduce-scatter.7
  710.0 24.2 all-gather.13
